TPU v7x, 768 devices: a whole 4x8x12 slice. The times are simulated.
768 devices in a mesh: lon: 8 (over y_lo, core), lat: 96 (over x, y_hi, z).
Axes of the slice: x: 4, y: 8 (y_hi: 2, y_lo: 4; y = y_hi * 4 + y_lo), z: 12, core: 2. Of those that a mesh axis runs over, the one named last changes fastest.
Arguments:
- forcing: float32 [8, 2304, 4096], P(None, 'lat', 'lon'), may hold values from -6 to 6
- kappa_lon: float32 [8, 2304, 4096], P(None, 'lat', 'lon'), may hold values from 0.025 to 0.2
- kappa_lat: float32 [8, 2304, 4096], P(None, 'lat', 'lon'), may hold values from 0.025 to 0.2
- shear: float32 [8, 2304, 4096], P(None, 'lat', 'lon'), may hold values from -0.8 to 0.8
- amplitude: float32 [8, 2304, 4096], P(None, 'lat', 'lon'), may hold values from 0.5 to 2
- tile_owner: int32 [2304, 32], P('lat', 'lon'), may hold values from -1 to 7, as said below
Outputs:
- packed: float32 [96, 768, 8, 128], P('lat', 'lon')
Inputs may be any that keep to these rules, and one draw needn't show every extreme that they name: `tile_owner`: owners lie in the same device row of lat. From the tiles of one device at most 12 go to one owner, and in every device row one owner receives exactly 12 tiles from each device of that row.
All inputs are finite; a program needn't handle non-finite values.
Results may differ from a plain program's by a relative error of at most 0.00015.
Values sent between devices are 32-bit elements; how exact they have to be, the bound alone decides.
A program may use at most 32 MiB of HBM per device.

v0:
```python
import jax
import jax.numpy as jnp
from jax import lax
from jax.sharding import PartitionSpec as P

ITERS = 6


def padded(cells, sides, width, closed):
    for axis, dim in sides:
        count = lax.axis_size(axis)
        ends = count if closed else count - 1
        head = lax.slice_in_dim(cells, 0, width, axis=dim)
        tail = lax.slice_in_dim(cells, cells.shape[dim] - width, cells.shape[dim], axis=dim)
        cells = jnp.concatenate(
            [
                lax.ppermute(tail, axis, [(i, (i + 1) % count) for i in range(ends)]),
                cells,
                lax.ppermute(head, axis, [((i + 1) % count, i) for i in range(ends)]),
            ],
            axis=dim,
        )
    return cells


def from_partner(value, axis, distance):
    mask = 2**distance
    pairs = [(source, source ^ mask) for source in range(lax.axis_size(axis))]
    return lax.ppermute(value, axis, pairs)


def diffuse(state_field, kappa_lon, kappa_lat, cross_term, ocean_mask):
    centre = state_field[:, 1:-1, 1:-1]
    east_cell = state_field[:, 1:-1, 2:]
    west_cell = state_field[:, 1:-1, :-2]
    north_cell = state_field[:, 2:, 1:-1]
    south_cell = state_field[:, :-2, 1:-1]
    upper_east = state_field[:, 2:, 2:]
    upper_west = state_field[:, 2:, :-2]
    lower_east = state_field[:, :-2, 2:]
    lower_west = state_field[:, :-2, :-2]
    change = kappa_lon * (east_cell + west_cell - 2.0 * centre)
    change = change + kappa_lat * (north_cell + south_cell - 2.0 * centre)
    change = change + cross_term * (upper_east - upper_west - lower_east + lower_west)
    return centre + ocean_mask * change


def extend(source, rim_width):
    lat_grown = padded(source, (("lat", 1),), rim_width, False)
    top_rows = source[:, source.shape[1] - rim_width :, :]
    partner = top_rows
    for bit_index in range(lax.axis_size("lon").bit_length() - 1):
        partner = from_partner(partner, "lon", bit_index)
    mirror_rows = jnp.flip(partner, axis=(1, 2))
    is_top = lax.axis_index("lat") == lax.axis_size("lat") - 1
    upper_rim = jnp.where(is_top, mirror_rows, lat_grown[:, lat_grown.shape[1] - rim_width :, :])
    lat_grown = jnp.concatenate(
        [lat_grown[:, : lat_grown.shape[1] - rim_width, :], upper_rim], axis=1
    )
    return padded(lat_grown, (("lon", 2),), rim_width, True)


def per_device(forcing, kappa_lon, kappa_lat, shear, amplitude, tile_owner):
    levels = forcing.shape[0]
    lon_cells = forcing.shape[2]
    tile_cells = lon_cells // tile_owner.shape[1]
    tiles_device = tile_owner.shape[0] * tile_owner.shape[1]
    ocean = (tile_owner >= 0).astype(jnp.float32)
    ocean_mask = jnp.repeat(ocean, tile_cells, axis=1)[None]
    cross_term = 0.5 * shear * jnp.sqrt(kappa_lon * kappa_lat)
    state_field = ocean_mask * forcing
    halo_depth = 1
    coef_list = (kappa_lon, kappa_lat, cross_term, ocean_mask)
    for round_index in range(ITERS // halo_depth):
        extended = extend(state_field, halo_depth)
        extended = diffuse(extended, coef_list[0], coef_list[1], coef_list[2], coef_list[3])
        state_field = extended
    sample = amplitude * state_field
    tile_data = sample.reshape(
        levels, tile_owner.shape[0], tile_owner.shape[1], tile_cells
    ).transpose(1, 2, 0, 3)
    tile_data = tile_data.reshape(tiles_device, levels, tile_cells)
    owner_flat = tile_owner.reshape(tiles_device)
    owners_count = lax.axis_size("lon")
    slot_most = tiles_device // owners_count
    onehot = (owner_flat[:, None] == jnp.arange(owners_count, dtype=jnp.int32)[None, :]).astype(
        jnp.int32
    )
    rank_slot = jnp.sum((jnp.cumsum(onehot, axis=0) - 1) * onehot, axis=1)
    slot_index = jnp.where(owner_flat >= 0, owner_flat * slot_most + rank_slot, -1)
    select = (
        slot_index[None, :] == jnp.arange(owners_count * slot_most, dtype=jnp.int32)[:, None]
    ).astype(jnp.float32)
    outgoing = jnp.einsum("st,tlw->slw", select, tile_data, precision=lax.Precision.HIGHEST)
    return lax.all_to_all(outgoing[None], "lon", split_axis=1, concat_axis=1, tiled=True)


def solution(mesh):
    return jax.shard_map(
        per_device,
        mesh=mesh,
        in_specs=(
            P(None, "lat", "lon"),
            P(None, "lat", "lon"),
            P(None, "lat", "lon"),
            P(None, "lat", "lon"),
            P(None, "lat", "lon"),
            P("lat", "lon"),
        ),
        out_specs=P("lat", "lon", None, None),
        check_vma=False,
    )
```

profile of v0, /device:TPU:6, one launch (start us, length us, event | category | flops | bytes accessed | tf_op | source)
XLA Modules:
  0.0 256.7 jit_solution(4536471812456835885)
XLA Ops:
  5.0 3.5 %collective-permute-start.2 = (f32[8,1,512]{2,1,0:T(1,128)S(1)}, f32[8,1,512]{2,1,0:T(1,128)S(1)}, u32[]{:S(2)}, u32[]{:S(2)}) collective-permute-start(f32[8,1,512]{2,1,0:T(1,128)S(1)} %collective-permute-done.1), channel_id=1, source_target_pairs={{0,192},{96,288},{192,0},{288,96},{384,576},{480,672},{576,384},{6... | collective-permute-start | bytes 49160 | tf_op jit(solution)/shard_map/ppermute | solution.py:29
  10.6 4.5 %collective-permute-start.3 = (f32[8,1,512]{2,1,0:T(1,128)S(1)}, f32[8,1,512]{2,1,0:T(1,128)S(1)}, u32[]{:S(2)}, u32[]{:S(2)}) collective-permute-start(f32[8,1,512]{2,1,0:T(1,128)S(1)} %collective-permute-done.2), channel_id=1, source_target_pairs={{0,384},{96,480},{192,576},{288,672},{384,0},{480,96},{576,192},{6... | collective-permute-start | bytes 49160 | tf_op jit(solution)/shard_map/ppermute | solution.py:29
  15.1 18.3 %collective-permute-start.4 = (f32[8,1,512]{2,1,0:T(1,128)S(1)}, f32[8,1,512]{2,1,0:T(1,128)S(1)}, u32[]{:S(2)}, u32[]{:S(2)}) collective-permute-start(f32[8,1,512]{2,1,0:T(1,128)S(1)} %get-tuple-element.39), channel_id=1, source_target_pairs={{1,0},{2,1},{3,2},{4,3},{5,4},{6,5},{7,6},{8,7},{9,8},{10,9},{11,1... | collective-permute-start | bytes 49160 | tf_op jit(solution)/shard_map/ppermute | solution.py:19
  36.0 10.1 %collective-permute-done = f32[8,1,512]{2,1,0:T(1,128)S(1)} collective-permute-done((f32[8,1,512]{2,1,0:T(1,128)S(1)}, f32[8,1,512]{2,1,0:T(1,128)S(1)}, u32[]{:S(2)}, u32[]{:S(2)}) %collective-permute-start) | collective-permute-done | bytes 16416 | tf_op jit(solution)/shard_map/ppermute | solution.py:17
  50.6 5.7 %collective-permute-done.6 = f32[8,26,1]{2,1,0:T(8,128)S(1)} collective-permute-done((f32[8,26,1]{2,1,0:T(8,128)S(1)}, f32[8,26,1]{2,1,0:T(8,128)S(1)}, u32[]{:S(2)}, u32[]{:S(2)}) %collective-permute-start.6) | collective-permute-done | bytes 864 | tf_op jit(solution)/shard_map/ppermute | solution.py:17
  62.4 3.7 %collective-permute-done.9 = f32[8,1,512]{2,1,0:T(1,128)S(1)} collective-permute-done((f32[8,1,512]{2,1,0:T(1,128)S(1)}, f32[8,1,512]{2,1,0:T(1,128)S(1)}, u32[]{:S(2)}, u32[]{:S(2)}) %collective-permute-start.9) | collective-permute-done | bytes 16416 | tf_op jit(solution)/shard_map/ppermute | solution.py:29
  70.3 3.9 %collective-permute-start.7 = (f32[8,1,512]{2,1,0:T(1,128)S(1)}, f32[8,1,512]{2,1,0:T(1,128)S(1)}, u32[]{:S(2)}, u32[]{:S(2)}) collective-permute-start(f32[8,1,512]{2,1,0:T(1,128)S(1)} %get-tuple-element.38), channel_id=1, source_target_pairs={{0,1},{1,2},{2,3},{3,4},{4,5},{5,6},{6,7},{7,8},{8,9},{9,10},{10,1... | collective-permute-start | bytes 49160 | tf_op jit(solution)/shard_map/ppermute | solution.py:17
  74.7 8.1 %collective-permute-done.7 = f32[8,1,512]{2,1,0:T(1,128)S(1)} collective-permute-done((f32[8,1,512]{2,1,0:T(1,128)S(1)}, f32[8,1,512]{2,1,0:T(1,128)S(1)}, u32[]{:S(2)}, u32[]{:S(2)}) %collective-permute-start.7) | collective-permute-done | bytes 16416 | tf_op jit(solution)/shard_map/ppermute | solution.py:17
  87.4 5.6 %collective-permute-done.13 = f32[8,26,1]{2,1,0:T(8,128)S(1)} collective-permute-done((f32[8,26,1]{2,1,0:T(8,128)S(1)}, f32[8,26,1]{2,1,0:T(8,128)S(1)}, u32[]{:S(2)}, u32[]{:S(2)}) %collective-permute-start.13) | collective-permute-done | bytes 864 | tf_op jit(solution)/shard_map/ppermute | solution.py:17
  99.0 3.7 %collective-permute-done.16 = f32[8,1,512]{2,1,0:T(1,128)S(1)} collective-permute-done((f32[8,1,512]{2,1,0:T(1,128)S(1)}, f32[8,1,512]{2,1,0:T(1,128)S(1)}, u32[]{:S(2)}, u32[]{:S(2)}) %collective-permute-start.16) | collective-permute-done | bytes 16416 | tf_op jit(solution)/shard_map/ppermute | solution.py:29
  107.3 3.9 %collective-permute-start.14 = (f32[8,1,512]{2,1,0:T(1,128)S(1)}, f32[8,1,512]{2,1,0:T(1,128)S(1)}, u32[]{:S(2)}, u32[]{:S(2)}) collective-permute-start(f32[8,1,512]{2,1,0:T(1,128)S(1)} %get-tuple-element.36), channel_id=1, source_target_pairs={{0,1},{1,2},{2,3},{3,4},{4,5},{5,6},{6,7},{7,8},{8,9},{9,10},{10,1... | collective-permute-start | bytes 49160 | tf_op jit(solution)/shard_map/ppermute | solution.py:17
  111.8 8.1 %collective-permute-done.14 = f32[8,1,512]{2,1,0:T(1,128)S(1)} collective-permute-done((f32[8,1,512]{2,1,0:T(1,128)S(1)}, f32[8,1,512]{2,1,0:T(1,128)S(1)}, u32[]{:S(2)}, u32[]{:S(2)}) %collective-permute-start.14) | collective-permute-done | bytes 16416 | tf_op jit(solution)/shard_map/ppermute | solution.py:17
  124.4 5.6 %collective-permute-done.20 = f32[8,26,1]{2,1,0:T(8,128)S(1)} collective-permute-done((f32[8,26,1]{2,1,0:T(8,128)S(1)}, f32[8,26,1]{2,1,0:T(8,128)S(1)}, u32[]{:S(2)}, u32[]{:S(2)}) %collective-permute-start.20) | collective-permute-done | bytes 864 | tf_op jit(solution)/shard_map/ppermute | solution.py:17
  136.1 3.7 %collective-permute-done.23 = f32[8,1,512]{2,1,0:T(1,128)S(1)} collective-permute-done((f32[8,1,512]{2,1,0:T(1,128)S(1)}, f32[8,1,512]{2,1,0:T(1,128)S(1)}, u32[]{:S(2)}, u32[]{:S(2)}) %collective-permute-start.23) | collective-permute-done | bytes 16416 | tf_op jit(solution)/shard_map/ppermute | solution.py:29
  143.9 3.9 %collective-permute-start.21 = (f32[8,1,512]{2,1,0:T(1,128)S(1)}, f32[8,1,512]{2,1,0:T(1,128)S(1)}, u32[]{:S(2)}, u32[]{:S(2)}) collective-permute-start(f32[8,1,512]{2,1,0:T(1,128)S(1)} %get-tuple-element.34), channel_id=1, source_target_pairs={{0,1},{1,2},{2,3},{3,4},{4,5},{5,6},{6,7},{7,8},{8,9},{9,10},{10,1... | collective-permute-start | bytes 49160 | tf_op jit(solution)/shard_map/ppermute | solution.py:17
  148.4 8.1 %collective-permute-done.21 = f32[8,1,512]{2,1,0:T(1,128)S(1)} collective-permute-done((f32[8,1,512]{2,1,0:T(1,128)S(1)}, f32[8,1,512]{2,1,0:T(1,128)S(1)}, u32[]{:S(2)}, u32[]{:S(2)}) %collective-permute-start.21) | collective-permute-done | bytes 16416 | tf_op jit(solution)/shard_map/ppermute | solution.py:17
  161.0 5.6 %collective-permute-done.27 = f32[8,26,1]{2,1,0:T(8,128)S(1)} collective-permute-done((f32[8,26,1]{2,1,0:T(8,128)S(1)}, f32[8,26,1]{2,1,0:T(8,128)S(1)}, u32[]{:S(2)}, u32[]{:S(2)}) %collective-permute-start.27) | collective-permute-done | bytes 864 | tf_op jit(solution)/shard_map/ppermute | solution.py:17
  172.7 3.7 %collective-permute-done.30 = f32[8,1,512]{2,1,0:T(1,128)S(1)} collective-permute-done((f32[8,1,512]{2,1,0:T(1,128)S(1)}, f32[8,1,512]{2,1,0:T(1,128)S(1)}, u32[]{:S(2)}, u32[]{:S(2)}) %collective-permute-start.30) | collective-permute-done | bytes 16416 | tf_op jit(solution)/shard_map/ppermute | solution.py:29
  181.0 3.9 %collective-permute-start.28 = (f32[8,1,512]{2,1,0:T(1,128)S(1)}, f32[8,1,512]{2,1,0:T(1,128)S(1)}, u32[]{:S(2)}, u32[]{:S(2)}) collective-permute-start(f32[8,1,512]{2,1,0:T(1,128)S(1)} %get-tuple-element.32), channel_id=1, source_target_pairs={{0,1},{1,2},{2,3},{3,4},{4,5},{5,6},{6,7},{7,8},{8,9},{9,10},{10,1... | collective-permute-start | bytes 49160 | tf_op jit(solution)/shard_map/ppermute | solution.py:17
  185.5 8.1 %collective-permute-done.28 = f32[8,1,512]{2,1,0:T(1,128)S(1)} collective-permute-done((f32[8,1,512]{2,1,0:T(1,128)S(1)}, f32[8,1,512]{2,1,0:T(1,128)S(1)}, u32[]{:S(2)}, u32[]{:S(2)}) %collective-permute-start.28) | collective-permute-done | bytes 16416 | tf_op jit(solution)/shard_map/ppermute | solution.py:17
  198.1 5.6 %collective-permute-done.34 = f32[8,26,1]{2,1,0:T(8,128)S(1)} collective-permute-done((f32[8,26,1]{2,1,0:T(8,128)S(1)}, f32[8,26,1]{2,1,0:T(8,128)S(1)}, u32[]{:S(2)}, u32[]{:S(2)}) %collective-permute-start.34) | collective-permute-done | bytes 864 | tf_op jit(solution)/shard_map/ppermute | solution.py:17
  220.7 7.7 %collective-permute-done.35 = f32[8,1,512]{2,1,0:T(1,128)S(1)} collective-permute-done((f32[8,1,512]{2,1,0:T(1,128)S(1)}, f32[8,1,512]{2,1,0:T(1,128)S(1)}, u32[]{:S(2)}, u32[]{:S(2)}) %collective-permute-start.35) | collective-permute-done | bytes 16416 | tf_op jit(solution)/shard_map/ppermute | solution.py:17
  233.8 5.4 %collective-permute-done.41 = f32[8,26,1]{2,1,0:T(8,128)S(1)} collective-permute-done((f32[8,26,1]{2,1,0:T(8,128)S(1)}, f32[8,26,1]{2,1,0:T(8,128)S(1)}, u32[]{:S(2)}, u32[]{:S(2)}) %collective-permute-start.41) | collective-permute-done | bytes 864 | tf_op jit(solution)/shard_map/ppermute | solution.py:17
  241.0 14.9 %all_to_all.5 = f32[1,96,8,128]{3,2,0,1:T(8,128)S(1)} all-to-all(f32[1,96,8,128]{3,2,0,1:T(8,128)S(1)} %copy.15), channel_id=1, replica_groups=mesh['lon'=8,'lat'=96] {'lon'}, dimensions={1} | all-to-all | bytes 786432 | tf_op jit(solution)/shard_map/all_to_all | solution.py:95
  (122 shorter events, 100.7 us)
Async XLA Ops:
  10.6 24.8 %collective-permute-start.3 = (f32[8,1,512]{2,1,0:T(1,128)S(1)}, f32[8,1,512]{2,1,0:T(1,128)S(1)}, u32[]{:S(2)}, u32[]{:S(2)}) collective-permute-start(f32[8,1,512]{2,1,0:T(1,128)S(1)} %collective-permute-done.2), channel_id=1, source_target_pairs={{0,384},{96,480},{192,576},{288,672},{384,0},{480,96},{576,192},{6... | collective-permute-start | bytes 49160 | tf_op jit(solution)/shard_map/ppermute | solution.py:29
  15.1 20.8 %collective-permute-start.4 = (f32[8,1,512]{2,1,0:T(1,128)S(1)}, f32[8,1,512]{2,1,0:T(1,128)S(1)}, u32[]{:S(2)}, u32[]{:S(2)}) collective-permute-start(f32[8,1,512]{2,1,0:T(1,128)S(1)} %get-tuple-element.39), channel_id=1, source_target_pairs={{1,0},{2,1},{3,2},{4,3},{5,4},{6,5},{7,6},{8,7},{9,8},{10,9},{11,1... | collective-permute-start | bytes 49160 | tf_op jit(solution)/shard_map/ppermute | solution.py:19
  33.5 12.5 %collective-permute-start = (f32[8,1,512]{2,1,0:T(1,128)S(1)}, f32[8,1,512]{2,1,0:T(1,128)S(1)}, u32[]{:S(2)}, u32[]{:S(2)}) collective-permute-start(f32[8,1,512]{2,1,0:T(1,128)S(1)} %get-tuple-element.40), channel_id=1, source_target_pairs={{0,1},{1,2},{2,3},{3,4},{4,5},{5,6},{6,7},{7,8},{8,9},{9,10},{10,1... | collective-permute-start | bytes 49160 | tf_op jit(solution)/shard_map/ppermute | solution.py:17
  48.1 8.2 %collective-permute-start.6 = (f32[8,26,1]{2,1,0:T(8,128)S(1)}, f32[8,26,1]{2,1,0:T(8,128)S(1)}, u32[]{:S(2)}, u32[]{:S(2)}) collective-permute-start(f32[8,26,1]{2,1,0:T(8,128)S(1)} %get-tuple-element.28), channel_id=1, source_target_pairs={{0,96},{96,192},{192,288},{288,384},{384,480},{480,576},{576,672},... | collective-permute-start | bytes 2504 | tf_op jit(solution)/shard_map/ppermute | solution.py:17
  66.1 8.1 %collective-permute-start.10 = (f32[8,1,512]{2,1,0:T(1,128)S(1)}, f32[8,1,512]{2,1,0:T(1,128)S(1)}, u32[]{:S(2)}, u32[]{:S(2)}) collective-permute-start(f32[8,1,512]{2,1,0:T(1,128)S(1)} %collective-permute-done.9), channel_id=1, source_target_pairs={{0,384},{96,480},{192,576},{288,672},{384,0},{480,96},{576,192},{6... | collective-permute-start | bytes 49160 | tf_op jit(solution)/shard_map/ppermute | solution.py:29
  68.3 6.4 %collective-permute-start.11 = (f32[8,1,512]{2,1,0:T(1,128)S(1)}, f32[8,1,512]{2,1,0:T(1,128)S(1)}, u32[]{:S(2)}, u32[]{:S(2)}) collective-permute-start(f32[8,1,512]{2,1,0:T(1,128)S(1)} %get-tuple-element.37), channel_id=1, source_target_pairs={{1,0},{2,1},{3,2},{4,3},{5,4},{6,5},{7,6},{8,7},{9,8},{10,9},{11,1... | collective-permute-start | bytes 49160 | tf_op jit(solution)/shard_map/ppermute | solution.py:19
  70.3 12.5 %collective-permute-start.7 = (f32[8,1,512]{2,1,0:T(1,128)S(1)}, f32[8,1,512]{2,1,0:T(1,128)S(1)}, u32[]{:S(2)}, u32[]{:S(2)}) collective-permute-start(f32[8,1,512]{2,1,0:T(1,128)S(1)} %get-tuple-element.38), channel_id=1, source_target_pairs={{0,1},{1,2},{2,3},{3,4},{4,5},{5,6},{6,7},{7,8},{8,9},{9,10},{10,1... | collective-permute-start | bytes 49160 | tf_op jit(solution)/shard_map/ppermute | solution.py:17
  84.9 8.1 %collective-permute-start.13 = (f32[8,26,1]{2,1,0:T(8,128)S(1)}, f32[8,26,1]{2,1,0:T(8,128)S(1)}, u32[]{:S(2)}, u32[]{:S(2)}) collective-permute-start(f32[8,26,1]{2,1,0:T(8,128)S(1)} %get-tuple-element.24), channel_id=1, source_target_pairs={{0,96},{96,192},{192,288},{288,384},{384,480},{480,576},{576,672},... | collective-permute-start | bytes 2504 | tf_op jit(solution)/shard_map/ppermute | solution.py:17
  102.7 8.6 %collective-permute-start.17 = (f32[8,1,512]{2,1,0:T(1,128)S(1)}, f32[8,1,512]{2,1,0:T(1,128)S(1)}, u32[]{:S(2)}, u32[]{:S(2)}) collective-permute-start(f32[8,1,512]{2,1,0:T(1,128)S(1)} %collective-permute-done.16), channel_id=1, source_target_pairs={{0,384},{96,480},{192,576},{288,672},{384,0},{480,96},{576,192},{6... | collective-permute-start | bytes 49160 | tf_op jit(solution)/shard_map/ppermute | solution.py:29
  105.4 6.4 %collective-permute-start.18 = (f32[8,1,512]{2,1,0:T(1,128)S(1)}, f32[8,1,512]{2,1,0:T(1,128)S(1)}, u32[]{:S(2)}, u32[]{:S(2)}) collective-permute-start(f32[8,1,512]{2,1,0:T(1,128)S(1)} %get-tuple-element.35), channel_id=1, source_target_pairs={{1,0},{2,1},{3,2},{4,3},{5,4},{6,5},{7,6},{8,7},{9,8},{10,9},{11,1... | collective-permute-start | bytes 49160 | tf_op jit(solution)/shard_map/ppermute | solution.py:19
  107.3 12.5 %collective-permute-start.14 = (f32[8,1,512]{2,1,0:T(1,128)S(1)}, f32[8,1,512]{2,1,0:T(1,128)S(1)}, u32[]{:S(2)}, u32[]{:S(2)}) collective-permute-start(f32[8,1,512]{2,1,0:T(1,128)S(1)} %get-tuple-element.36), channel_id=1, source_target_pairs={{0,1},{1,2},{2,3},{3,4},{4,5},{5,6},{6,7},{7,8},{8,9},{9,10},{10,1... | collective-permute-start | bytes 49160 | tf_op jit(solution)/shard_map/ppermute | solution.py:17
  121.9 8.1 %collective-permute-start.20 = (f32[8,26,1]{2,1,0:T(8,128)S(1)}, f32[8,26,1]{2,1,0:T(8,128)S(1)}, u32[]{:S(2)}, u32[]{:S(2)}) collective-permute-start(f32[8,26,1]{2,1,0:T(8,128)S(1)} %get-tuple-element.20), channel_id=1, source_target_pairs={{0,96},{96,192},{192,288},{288,384},{384,480},{480,576},{576,672},... | collective-permute-start | bytes 2504 | tf_op jit(solution)/shard_map/ppermute | solution.py:17
  139.8 8.1 %collective-permute-start.24 = (f32[8,1,512]{2,1,0:T(1,128)S(1)}, f32[8,1,512]{2,1,0:T(1,128)S(1)}, u32[]{:S(2)}, u32[]{:S(2)}) collective-permute-start(f32[8,1,512]{2,1,0:T(1,128)S(1)} %collective-permute-done.23), channel_id=1, source_target_pairs={{0,384},{96,480},{192,576},{288,672},{384,0},{480,96},{576,192},{6... | collective-permute-start | bytes 49160 | tf_op jit(solution)/shard_map/ppermute | solution.py:29
  142.0 6.4 %collective-permute-start.25 = (f32[8,1,512]{2,1,0:T(1,128)S(1)}, f32[8,1,512]{2,1,0:T(1,128)S(1)}, u32[]{:S(2)}, u32[]{:S(2)}) collective-permute-start(f32[8,1,512]{2,1,0:T(1,128)S(1)} %get-tuple-element.33), channel_id=1, source_target_pairs={{1,0},{2,1},{3,2},{4,3},{5,4},{6,5},{7,6},{8,7},{9,8},{10,9},{11,1... | collective-permute-start | bytes 49160 | tf_op jit(solution)/shard_map/ppermute | solution.py:19
  143.9 12.5 %collective-permute-start.21 = (f32[8,1,512]{2,1,0:T(1,128)S(1)}, f32[8,1,512]{2,1,0:T(1,128)S(1)}, u32[]{:S(2)}, u32[]{:S(2)}) collective-permute-start(f32[8,1,512]{2,1,0:T(1,128)S(1)} %get-tuple-element.34), channel_id=1, source_target_pairs={{0,1},{1,2},{2,3},{3,4},{4,5},{5,6},{6,7},{7,8},{8,9},{9,10},{10,1... | collective-permute-start | bytes 49160 | tf_op jit(solution)/shard_map/ppermute | solution.py:17
  158.5 8.1 %collective-permute-start.27 = (f32[8,26,1]{2,1,0:T(8,128)S(1)}, f32[8,26,1]{2,1,0:T(8,128)S(1)}, u32[]{:S(2)}, u32[]{:S(2)}) collective-permute-start(f32[8,26,1]{2,1,0:T(8,128)S(1)} %get-tuple-element.16), channel_id=1, source_target_pairs={{0,96},{96,192},{192,288},{288,384},{384,480},{480,576},{576,672},... | collective-permute-start | bytes 2504 | tf_op jit(solution)/shard_map/ppermute | solution.py:17
  176.4 8.6 %collective-permute-start.31 = (f32[8,1,512]{2,1,0:T(1,128)S(1)}, f32[8,1,512]{2,1,0:T(1,128)S(1)}, u32[]{:S(2)}, u32[]{:S(2)}) collective-permute-start(f32[8,1,512]{2,1,0:T(1,128)S(1)} %collective-permute-done.30), channel_id=1, source_target_pairs={{0,384},{96,480},{192,576},{288,672},{384,0},{480,96},{576,192},{6... | collective-permute-start | bytes 49160 | tf_op jit(solution)/shard_map/ppermute | solution.py:29
  179.1 6.4 %collective-permute-start.32 = (f32[8,1,512]{2,1,0:T(1,128)S(1)}, f32[8,1,512]{2,1,0:T(1,128)S(1)}, u32[]{:S(2)}, u32[]{:S(2)}) collective-permute-start(f32[8,1,512]{2,1,0:T(1,128)S(1)} %get-tuple-element.31), channel_id=1, source_target_pairs={{1,0},{2,1},{3,2},{4,3},{5,4},{6,5},{7,6},{8,7},{9,8},{10,9},{11,1... | collective-permute-start | bytes 49160 | tf_op jit(solution)/shard_map/ppermute | solution.py:19
  181.0 12.5 %collective-permute-start.28 = (f32[8,1,512]{2,1,0:T(1,128)S(1)}, f32[8,1,512]{2,1,0:T(1,128)S(1)}, u32[]{:S(2)}, u32[]{:S(2)}) collective-permute-start(f32[8,1,512]{2,1,0:T(1,128)S(1)} %get-tuple-element.32), channel_id=1, source_target_pairs={{0,1},{1,2},{2,3},{3,4},{4,5},{5,6},{6,7},{7,8},{8,9},{9,10},{10,1... | collective-permute-start | bytes 49160 | tf_op jit(solution)/shard_map/ppermute | solution.py:17
  195.6 8.1 %collective-permute-start.34 = (f32[8,26,1]{2,1,0:T(8,128)S(1)}, f32[8,26,1]{2,1,0:T(8,128)S(1)}, u32[]{:S(2)}, u32[]{:S(2)}) collective-permute-start(f32[8,26,1]{2,1,0:T(8,128)S(1)} %get-tuple-element.12), channel_id=1, source_target_pairs={{0,96},{96,192},{192,288},{288,384},{384,480},{480,576},{576,672},... | collective-permute-start | bytes 2504 | tf_op jit(solution)/shard_map/ppermute | solution.py:17
  210.0 10.7 %collective-permute-start.39 = (f32[8,1,512]{2,1,0:T(1,128)S(1)}, f32[8,1,512]{2,1,0:T(1,128)S(1)}, u32[]{:S(2)}, u32[]{:S(2)}) collective-permute-start(f32[8,1,512]{2,1,0:T(1,128)S(1)} %get-tuple-element.29), channel_id=1, source_target_pairs={{1,0},{2,1},{3,2},{4,3},{5,4},{6,5},{7,6},{8,7},{9,8},{10,9},{11,1... | collective-permute-start | bytes 49160 | tf_op jit(solution)/shard_map/ppermute | solution.py:19
  213.5 6.8 %collective-permute-start.38 = (f32[8,1,512]{2,1,0:T(1,128)S(1)}, f32[8,1,512]{2,1,0:T(1,128)S(1)}, u32[]{:S(2)}, u32[]{:S(2)}) collective-permute-start(f32[8,1,512]{2,1,0:T(1,128)S(1)} %collective-permute-done.37), channel_id=1, source_target_pairs={{0,384},{96,480},{192,576},{288,672},{384,0},{480,96},{576,192},{6... | collective-permute-start | bytes 49160 | tf_op jit(solution)/shard_map/ppermute | solution.py:29
  215.9 12.5 %collective-permute-start.35 = (f32[8,1,512]{2,1,0:T(1,128)S(1)}, f32[8,1,512]{2,1,0:T(1,128)S(1)}, u32[]{:S(2)}, u32[]{:S(2)}) collective-permute-start(f32[8,1,512]{2,1,0:T(1,128)S(1)} %get-tuple-element.30), channel_id=1, source_target_pairs={{0,1},{1,2},{2,3},{3,4},{4,5},{5,6},{6,7},{7,8},{8,9},{9,10},{10,1... | collective-permute-start | bytes 49160 | tf_op jit(solution)/shard_map/ppermute | solution.py:17
  231.1 8.1 %collective-permute-start.41 = (f32[8,26,1]{2,1,0:T(8,128)S(1)}, f32[8,26,1]{2,1,0:T(8,128)S(1)}, u32[]{:S(2)}, u32[]{:S(2)}) collective-permute-start(f32[8,26,1]{2,1,0:T(8,128)S(1)} %get-tuple-element.8), channel_id=1, source_target_pairs={{0,96},{96,192},{192,288},{288,384},{384,480},{480,576},{576,672},... | collective-permute-start | bytes 2504 | tf_op jit(solution)/shard_map/ppermute | solution.py:17
  (23 other events, 114.6 us)
where the time goes:
time: 258 us; the launch traced here: 257 us
  starting transfers between devices  116 us (45%)
  waiting for transfers between devices  111 us (43%)
  blocking collectives  14.9 us (6%)
  other arithmetic  8.93 us (3%)
  local copies, waits for them, and re-layouts  4.69 us (2%)
    ppermute x12, waiting for transfers between devices, padded(): lax.ppermute(tail, axis, [(i, (i + 1) % count) for i in range(ends)])  83.4 us
    ppermute x18, starting transfers between devices, from_partner(): return lax.ppermute(value, axis, pairs)  41.1 us
    ppermute x12, starting transfers between devices, padded(): lax.ppermute(head, axis, [((i + 1) % count, i) for i in range(ends)])  40.1 us
    ppermute x12, starting transfers between devices, padded(): lax.ppermute(tail, axis, [(i, (i + 1) % count) for i in range(ends)])  34.5 us
    ppermute x18, waiting for transfers between devices, from_partner(): return lax.ppermute(value, axis, pairs)  26.8 us
    all_to_all x1, blocking collectives, per_device(): lax.all_to_all(outgoing[None], 'lon', split_axis=1, concat_axis=1, tiled=...  14.9 us
  transfers between devices with their start and end apart: 42, of which 30 were waited for; matrix products, arithmetic and copies ran while one was open for 1% of the time, Pallas kernels for 0%

commit v1 on v0

v1 whole, which is shorter than its diff:
```python
import functools

import jax
import jax.numpy as jnp
from jax import lax
from jax.experimental import pallas as pl
from jax.experimental.pallas import tpu as pltpu
from jax.sharding import PartitionSpec as P

ITERS = 6
LEVELS = 8
WIDTH = 128
ROWS = 24
TILES = 4
RING = 5
GROUP = 8
TOTAL = ROWS + 2 * GROUP
OWNERS = 8
MOST = 12
PIECES = 2
MESH = pl.DeviceIdType.MESH


def lanes(shape=(LEVELS, WIDTH)):
    return lax.broadcasted_iota(jnp.int32, shape, len(shape) - 1)


def neighbours(row, lane):
    left = [pltpu.roll(v, WIDTH - 1, axis=1) for v in row]
    right = [pltpu.roll(v, 1, axis=1) for v in row]
    east = [jnp.where(lane == WIDTH - 1, left[(q + 1) % RING], left[q]) for q in range(RING)]
    west = [jnp.where(lane == 0, right[(q - 1) % RING], right[q]) for q in range(RING)]
    both = [e + w for e, w in zip(east, west)]
    slope = [e - w for e, w in zip(east, west)]
    return both, slope


def updated(coef, r, south, centre, north, lane_terms):
    south_slope, both, north_slope = lane_terms
    new = []
    for q in range(RING):
        twice = 2.0 * centre[q]
        change = coef[0, r, q] * (both[q] - twice)
        change = change + coef[1, r, q] * (north[q] + south[q] - twice)
        change = change + coef[2, r, q] * (north_slope[q] - south_slope[q])
        new.append(centre[q] + change)
    return new


def row_of(state, plane, r):
    return [state[plane, r, q] for q in range(RING)]


def sweep(state, coef, src, dst, low, count, below=None, above=None):
    lane = lanes()
    south = row_of(state, src, low - 1) if below is None else below
    centre = row_of(state, src, low)
    _, south_slope = neighbours(south, lane)
    both, slope = neighbours(centre, lane)

    def step(r, north, carry):
        south, south_slope, centre, both, slope = carry
        north_both, north_slope = neighbours(north, lane)
        new = updated(coef, r, south, centre, north, (south_slope, both, north_slope))
        for q in range(RING):
            state[dst, r, q] = new[q]
        return centre, slope, north, north_both, north_slope

    def body(i, carry):
        r = low + i
        return step(r, row_of(state, src, r + 1), carry)

    carry = (south, south_slope, centre, both, slope)
    if above is None:
        lax.fori_loop(0, count, body, carry)
    else:
        carry = lax.fori_loop(0, count - 1, body, carry)
        step(low + count - 1, above, carry)


def kernel(
    forcing, kappa_lon, kappa_lat, shear, amplitude, owner, out,
    raw, state, coef, scale, saved, lon_send, lon_recv, lat_recv, packed, index_v, index_s,
    load_sem, lon_ssem, lon_rsem, lat_ssem, lat_rsem, out_ssem, out_rsem, own_sem, index_sem,
):
    s = lax.axis_index("lon")
    a = lax.axis_index("lat")
    n_lon = lax.axis_size("lon")
    n_lat = lax.axis_size("lat")
    fold = a // (n_lat - 1)
    has_south = a > 0
    north_lon = s + fold * (n_lon - 1 - 2 * s)
    north_lat = a + 1 - fold
    east = lax.rem(s + 1, n_lon)
    west = lax.rem(s + n_lon - 1, n_lon)

    barrier = pltpu.get_barrier_semaphore()
    for d in range(1, OWNERS):
        pl.semaphore_signal(barrier, inc=1, device_id=(lax.rem(s + d, n_lon), a), device_id_type=MESH)

    @pl.when(fold == 0)
    def _():
        pl.semaphore_signal(barrier, inc=1, device_id=(s, a + 1), device_id_type=MESH)

    @pl.when(has_south)
    def _():
        pl.semaphore_signal(barrier, inc=1, device_id=(s, a - 1), device_id_type=MESH)

    loads = [
        pltpu.make_async_copy(ref.at[:, pl.ds(q * WIDTH, WIDTH)], raw.at[i, q], load_sem.at[i, q])
        for i, ref in enumerate((forcing, kappa_lon, kappa_lat, shear, amplitude))
        for q in range(TILES)
    ]
    for load in loads:
        load.start()
    for load in loads:
        load.wait()

    lane = lanes()

    def prepare(r, _):
        for q in range(TILES):
            rows = pl.ds(r, LEVELS, ROWS)
            sea = (owner[r, q] >= 0).astype(jnp.float32)
            k_lon = raw[1, q, rows]
            k_lat = raw[2, q, rows]
            cross = 0.5 * raw[3, q, rows] * jnp.sqrt(k_lon * k_lat)
            state[0, GROUP + r, q] = sea * raw[0, q, rows]
            coef[0, GROUP + r, q] = sea * k_lon
            coef[1, GROUP + r, q] = sea * k_lat
            coef[2, GROUP + r, q] = sea * cross
            scale[r, q] = raw[4, q, rows]
        return 0

    lax.fori_loop(0, ROWS, prepare, 0)

    def piece(kind, r, q):
        return state[0, r, q] if kind == 0 else coef[kind - 1, r, q]

    per_vector = WIDTH // GROUP

    def pack_group(g, _):
        for v in range(PIECES):
            to_west = jnp.zeros((LEVELS, WIDTH), jnp.float32)
            to_east = jnp.zeros((LEVELS, WIDTH), jnp.float32)
            for j in range(per_vector):
                rr, kind = divmod(v * per_vector + j, 4)
                r = GROUP + g * GROUP + rr
                here = lane // GROUP == j
                first, last = piece(kind, r, 0), piece(kind, r, TILES - 1)
                if j:
                    first = pltpu.roll(first, GROUP * j, axis=1)
                if j < per_vector - 1:
                    last = pltpu.roll(last, GROUP * (j + 1), axis=1)
                to_west = jnp.where(here, first, to_west)
                to_east = jnp.where(here, last, to_east)
            lon_send[0, g, v] = to_west
            lon_send[1, g, v] = to_east
        return 0

    lax.fori_loop(0, ROWS // GROUP, pack_group, 0)

    def unpack(buf, g, base):
        for v in range(PIECES):
            from_east, from_west = buf[g, 0, v], buf[g, 1, v]
            for j in range(per_vector):
                rr, kind = divmod(v * per_vector + j, 4)
                after = from_east if j == 0 else pltpu.roll(from_east, WIDTH - GROUP * j, axis=1)
                before = from_west if j == per_vector - 1 else pltpu.roll(from_west, WIDTH - GROUP * (j + 1), axis=1)
                ends = jnp.where(lane < ITERS, after, jnp.where(lane >= WIDTH - ITERS, before, 0.0))
                if kind == 0:
                    state[0, base + rr, TILES] = ends
                else:
                    coef[kind - 1, base + rr, TILES] = ends

    def spread(t, vec):
        return jnp.where(lane == t, owner[t // TILES, lax.rem(t, TILES)], vec)

    owner_vec = lax.fori_loop(0, ROWS * TILES, spread, jnp.full((OWNERS, WIDTH), -1, jnp.int32))
    mine = owner_vec == lax.broadcasted_iota(jnp.int32, (OWNERS, WIDTH), 0)
    rank = mine.astype(jnp.int32)
    for shift in (1, 2, 4, 8, 16, 32, 64):
        rank = rank + jnp.where(lane >= shift, pltpu.roll(rank, shift, axis=1), 0)
    index = jnp.full((OWNERS, WIDTH), -1, jnp.int32)
    for k in range(MOST):
        place = jnp.sum(jnp.where(mine & (rank == k + 1), lane + 1, 0), axis=1, keepdims=True) - 1
        index = jnp.where(lane == k, place, index)
    index_v[...] = index
    index_copy = pltpu.make_async_copy(index_v, index_s, index_sem)
    index_copy.start()

    pl.semaphore_wait(barrier, OWNERS - 1 + (1 - fold) + (a + n_lat - 1) // n_lat)

    def remote(src, dst, ssem, rsem, lon, lat):
        return pltpu.make_async_remote_copy(
            src_ref=src, dst_ref=dst, send_sem=ssem, recv_sem=rsem, device_id=(lon, lat), device_id_type=MESH
        )

    main = pl.ds(0, TILES)
    up = fold * (ROWS + GROUP)
    top = GROUP + ROWS
    to_west = remote(lon_send.at[0], lon_recv.at[:, 0], lon_ssem.at[0], lon_rsem.at[0], west, a)
    to_east = remote(lon_send.at[1], lon_recv.at[:, 1], lon_ssem.at[1], lon_rsem.at[1], east, a)
    northward = [
        remote(
            state.at[0, pl.ds(top - ITERS, ITERS), main], state.at[0, pl.ds(up + GROUP - ITERS, ITERS), main],
            lat_ssem.at[0], lat_rsem.at[fold, 0], north_lon, north_lat,
        ),
        remote(
            coef.at[:, pl.ds(top - ITERS + 1, ITERS - 1), main], coef.at[:, pl.ds(up + GROUP - ITERS + 1, ITERS - 1), main],
            lat_ssem.at[1], lat_rsem.at[fold, 1], north_lon, north_lat,
        ),
        remote(lon_recv.at[ROWS // GROUP - 1], lat_recv.at[fold], lat_ssem.at[2], lat_rsem.at[fold, 2], north_lon, north_lat),
    ]
    south_lat = lax.rem(a + n_lat - 1, n_lat)
    southward = [
        remote(
            state.at[0, pl.ds(GROUP, ITERS), main], state.at[0, pl.ds(top, ITERS), main],
            lat_ssem.at[3], lat_rsem.at[1, 0], s, south_lat,
        ),
        remote(
            coef.at[:, pl.ds(GROUP, ITERS - 1), main], coef.at[:, pl.ds(top, ITERS - 1), main],
            lat_ssem.at[4], lat_rsem.at[1, 1], s, south_lat,
        ),
        remote(lon_recv.at[0], lat_recv.at[1], lat_ssem.at[5], lat_rsem.at[1, 2], s, south_lat),
    ]

    to_west.start()
    to_east.start()
    northward[0].start()
    northward[1].start()

    @pl.when(has_south)
    def _():
        southward[0].start()
        southward[1].start()

    to_west.wait_recv()
    to_east.wait_recv()
    northward[2].start()

    @pl.when(has_south)
    def _():
        southward[2].start()

    def unpack_own(g, _):
        unpack(lon_recv, g, GROUP + g * GROUP)
        return 0

    lax.fori_loop(0, ROWS // GROUP, unpack_own, 0)

    for turn in range(1, ITERS + 1):
        src = 0 if turn == 1 else 1
        for q in range(RING):
            saved[0, turn - 1, q] = state[src, GROUP + turn, q]
            saved[1, turn - 1, q] = state[src, top - 1 - turn, q]
        sweep(state, coef, src, 1, GROUP + turn, ROWS - 2 * turn)

    @pl.when(has_south)
    def _():
        for i in range(3):
            remote(
                (state.at[0, pl.ds(top - ITERS, ITERS), main], coef.at[:, pl.ds(top - ITERS + 1, ITERS - 1), main], lon_recv.at[0])[i],
                (
                    state.at[0, pl.ds(GROUP - ITERS, ITERS), main],
                    coef.at[:, pl.ds(GROUP - ITERS + 1, ITERS - 1), main],
                    lat_recv.at[0],
                )[i],
                lat_ssem.at[i], lat_rsem.at[0, i], north_lon, north_lat,
            ).wait_recv()
        unpack(lat_recv, 0, 0)

    @pl.when(a == 0)
    def _():
        zero = jnp.zeros((LEVELS, WIDTH), jnp.float32)

        def clear(r, _):
            for q in range(RING):
                state[0, r, q] = zero
                for kind in range(3):
                    coef[kind, r, q] = zero
            return 0

        lax.fori_loop(0, GROUP, clear, 0)

    def south_turn(turn, _):
        src = (turn + ITERS - 2) // ITERS
        above = [saved[0, turn - 1, q] for q in range(RING)]
        sweep(state, coef, src, 1, GROUP - ITERS + turn, ITERS, above=above)
        return 0

    lax.fori_loop(1, ITERS + 1, south_turn, 0)

    for copy in southward:
        copy.wait_recv()
    unpack(lat_recv, 1, top)

    @pl.when(fold == 1)
    def _():
        mirror = WIDTH - 1 - lane

        def flipped(value):
            return jnp.take_along_axis(value, mirror, axis=1)

        def swap(m, _):
            low, high = top + m, top + GROUP - 1 - m
            for get, put in [
                (lambda r, q: state[0, r, q], 0),
                (lambda r, q: coef[0, r, q], 1),
                (lambda r, q: coef[1, r, q], 2),
                (lambda r, q: coef[2, r, q], 3),
            ]:
                old_low = [get(low, q) for q in range(RING)]
                old_high = [get(high, q) for q in range(RING)]
                for q in range(RING):
                    p = TILES - 1 - q if q < TILES else q
                    for r, value in ((low, old_high[p]), (high, old_low[p])):
                        if put == 0:
                            state[0, r, q] = flipped(value)
                        else:
                            coef[put - 1, r, q] = flipped(value)
            return 0

        lax.fori_loop(0, GROUP // 2, swap, 0)

    def north_turn(turn, _):
        src = (turn + ITERS - 2) // ITERS
        below = [saved[1, turn - 1, q] for q in range(RING)]
        sweep(state, coef, src, 1, top - turn, ITERS, below=below)
        return 0

    lax.fori_loop(1, ITERS + 1, north_turn, 0)

    index_copy.wait()

    def fill(o):
        for k in range(MOST):
            t = index_s[o, k]
            r = jnp.maximum(t, 0) // TILES
            q = jnp.maximum(t, 0) - r * TILES
            tile = scale[r, q] * state[1, GROUP + r, q]
            packed[o * MOST + k] = jnp.where(t >= 0, tile, 0.0)

    def to_owner(o, d):
        block = pl.ds(o * MOST, MOST)
        slot = pl.ds(s * MOST, MOST)
        return remote(packed.at[block], out.at[0, slot], out_ssem.at[d], out_rsem.at[d], o, a)

    def give(d, _):
        o = lax.rem(s + d, n_lon)
        fill(o)
        to_owner(o, d).start()
        return 0

    lax.fori_loop(1, OWNERS, give, 0)
    fill(s)
    own = pltpu.make_async_copy(packed.at[pl.ds(s * MOST, MOST)], out.at[0, pl.ds(s * MOST, MOST)], own_sem)
    own.start()
    to_west.wait_send()
    to_east.wait_send()
    for copy in northward:
        copy.wait_send()

    @pl.when(has_south)
    def _():
        for copy in southward:
            copy.wait_send()

    own.wait()

    def finish(d, _):
        to_owner(lax.rem(s + d, n_lon), d).wait()
        return 0

    lax.fori_loop(1, OWNERS, finish, 0)


def per_device(forcing, kappa_lon, kappa_lat, shear, amplitude, tile_owner):
    flat = [v.reshape(LEVELS * ROWS, TILES * WIDTH) for v in (forcing, kappa_lon, kappa_lat, shear, amplitude)]
    vmem = functools.partial(pltpu.VMEM, dtype=jnp.float32)
    dma = pltpu.SemaphoreType.DMA
    return pl.pallas_call(
        kernel,
        out_shape=jax.ShapeDtypeStruct((1, OWNERS * MOST, LEVELS, WIDTH), jnp.float32),
        in_specs=[pl.BlockSpec(memory_space=pl.ANY)] * 5 + [pl.BlockSpec(memory_space=pltpu.SMEM)],
        out_specs=pl.BlockSpec(memory_space=pl.ANY),
        scratch_shapes=[
            vmem((5, TILES, LEVELS * ROWS, WIDTH)),
            vmem((2, TOTAL, RING, LEVELS, WIDTH)),
            vmem((3, TOTAL, RING, LEVELS, WIDTH)),
            vmem((ROWS, TILES, LEVELS, WIDTH)),
            vmem((2, ITERS, RING, LEVELS, WIDTH)),
            vmem((2, ROWS // GROUP, PIECES, LEVELS, WIDTH)),
            vmem((ROWS // GROUP, 2, PIECES, LEVELS, WIDTH)),
            vmem((2, 2, PIECES, LEVELS, WIDTH)),
            vmem((OWNERS * MOST, LEVELS, WIDTH)),
            pltpu.VMEM((OWNERS, WIDTH), jnp.int32),
            pltpu.SMEM((OWNERS, WIDTH), jnp.int32),
            dma((5, TILES)),
            dma((2,)),
            dma((2,)),
            dma((6,)),
            dma((2, 3)),
            dma((OWNERS,)),
            dma((OWNERS,)),
            dma,
            dma,
        ],
        compiler_params=pltpu.CompilerParams(collective_id=0, has_side_effects=True),
    )(*flat, tile_owner)


def solution(mesh):
    return jax.shard_map(
        per_device,
        mesh=mesh,
        in_specs=(P(None, "lat", "lon"),) * 5 + (P("lat", "lon"),),
        out_specs=P("lat", "lon", None, None),
        check_vma=False,
    )
```

time: 258 us -> 65.3 us (0.25)
  the two profiles are of different devices: /device:TPU:6 before, /device:TPU:29 now
where the time goes in v1:
time: 65.3 us; the launch traced here: 65 us
  Pallas kernels  61.9 us (95%)
  local copies, waits for them, and re-layouts  3.13 us (5%)
    pallas_call x1, Pallas kernels, per_device(): pl.pallas_call(kernel, out_shape=jax.ShapeDtypeStruct((1, OWNERS * MOST,...  61.9 us
    unnamed x4, local copies, waits for them, and re-layouts  3.13 us

profile of v1, /device:TPU:29, one launch (start us, length us, event | category | flops | bytes accessed | tf_op | source)
XLA Modules:
  0.0 65.0 jit_solution(13897979213555022835)
XLA Ops:
  0.0 0.0 copy-start
  0.0 0.7 %copy-done = s32[24,4]{0,1:T(4,128)S(1)} copy-done((s32[24,4]{0,1:T(4,128)S(1)}, s32[24,4]{0,1:T(4,128)}, u32[]{:S(2)}) %copy-start) | copy-done | bytes 408
  0.7 0.7 %copy.7.owner = s32[24,4]{1,0:T(8,128)} copy(s32[24,4]{0,1:T(4,128)S(1)} %copy-done) | data formatting | bytes 768 | tf_op args[5]
  1.4 61.9 %shard_map.64 = f32[1,96,8,128]{3,2,1,0:T(8,128)} custom-call(f32[192,512]{1,0:T(8,128)} %bitcast.5, f32[192,512]{1,0:T(8,128)} %bitcast.6, f32[192,512]{1,0:T(8,128)} %bitcast.7, f32[192,512]{1,0:T(8,128)} %bitcast.8, f32[192,512]{1,0:T(8,128)} %bitcast.9, s32[24,4]{1,0:T(8,128)} %copy.7.owner), custom_call_target="tpu_custom_call" | custom-call | tf_op jit(solution)/shard_map/pallas_call | solution.py:382
  63.3 1.8 %copy.9 = f32[1,96,8,128]{3,2,1,0:T(8,128)} copy(f32[1,96,8,128]{3,2,1,0:T(8,128)} %shard_map.64) | data formatting | bytes 786432
Async XLA Ops:
  0.0 0.7 %copy-start = (s32[24,4]{0,1:T(4,128)S(1)}, s32[24,4]{0,1:T(4,128)}, u32[]{:S(2)}) copy-start(s32[24,4]{0,1:T(4,128)} %param.11) | copy-start | bytes 1156

commit v2 on v1

v2 whole, which is shorter than its diff:
```python
import functools

import jax
import jax.numpy as jnp
from jax import lax
from jax.experimental import pallas as pl
from jax.experimental.pallas import tpu as pltpu
from jax.sharding import PartitionSpec as P

ITERS = 6
LEVELS = 8
WIDTH = 128
ROWS = 24
TILES = 4
RING = 5
GROUP = 8
TOTAL = ROWS + 2 * GROUP
OWNERS = 8
MOST = 12
CHIPS_Z = 12
PIECES = 2
MESH = pl.DeviceIdType.MESH


def lanes(shape=(LEVELS, WIDTH)):
    return lax.broadcasted_iota(jnp.int32, shape, len(shape) - 1)


def neighbours(row, lane):
    left = [pltpu.roll(v, WIDTH - 1, axis=1) for v in row]
    right = [pltpu.roll(v, 1, axis=1) for v in row]
    east = [jnp.where(lane == WIDTH - 1, left[(q + 1) % RING], left[q]) for q in range(RING)]
    west = [jnp.where(lane == 0, right[(q - 1) % RING], right[q]) for q in range(RING)]
    both = [e + w for e, w in zip(east, west)]
    slope = [e - w for e, w in zip(east, west)]
    return both, slope


def updated(field, r, south, centre, north, lane_terms, sign):
    south_slope, both, north_slope = lane_terms
    new = []
    for q in range(RING):
        twice = 2.0 * centre[q]
        change = field[r, 1, q] * (both[q] - twice)
        change = change + field[r, 2, q] * (north[q] + south[q] - twice)
        cross = north_slope[q] - south_slope[q]
        change = change + field[r, 3, q] * (cross if sign is None else sign * cross)
        new.append(centre[q] + change)
    return new


def row_of(field, later, turn, r):
    return [field[r, 0, q] if turn == 0 else later[(turn - 1) % 2, r, q] for q in range(RING)]


def store(later, turn, r, new):
    for q in range(RING):
        later[(turn - 1) % 2, r, q] = new[q]


def sweep(field, later, turn, low, count):
    lane = lanes()
    south = row_of(field, later, turn - 1, low - 1)
    centre = row_of(field, later, turn - 1, low)
    _, south_slope = neighbours(south, lane)
    both, slope = neighbours(centre, lane)

    def body(i, carry):
        south, south_slope, centre, both, slope = carry
        r = low + i
        north = row_of(field, later, turn - 1, r + 1)
        north_both, north_slope = neighbours(north, lane)
        store(later, turn, r, updated(field, r, south, centre, north, (south_slope, both, north_slope), None))
        return centre, slope, north, north_both, north_slope

    lax.fori_loop(0, count, body, (south, south_slope, centre, both, slope), unroll=2)


def diagonal(field, later, start, step, sign):
    lane = lanes()
    outer = row_of(field, later, 0, start - step)
    for turn in range(1, ITERS + 1):
        r = start + step * (turn - 1)
        centre = row_of(field, later, turn - 1, r)
        inner = row_of(field, later, turn - 1, r + step)
        both, _ = neighbours(centre, lane)
        _, inner_slope = neighbours(inner, lane)
        _, outer_slope = neighbours(outer, lane)
        outer = updated(field, r, outer, centre, inner, (outer_slope, both, inner_slope), sign)
        store(later, turn, r, outer)


def kernel(
    forcing, kappa_lon, kappa_lat, shear, amplitude, owner, out,
    raw, field, later, scale, stage, stage_ends, lon_send, lon_recv, lat_recv, packed, owner_s, owner_v, index_v, index_s,
    load_sem, owner_sem, ready_sem, lon_ssem, lon_rsem, north_ssem, relay_ssem, south_ssem, lat_rsem,
    ends_ssem, ends_rsem, stage_rsem, forward_ssem, out_ssem, out_rsem, own_sem, index_sem,
):
    s = lax.axis_index("lon")
    a = lax.axis_index("lat")
    n_lon = lax.axis_size("lon")
    n_lat = lax.axis_size("lat")
    along = lax.rem(a, CHIPS_Z)
    fold = a // (n_lat - 1)
    has_south = (a + n_lat - 1) // n_lat
    wrap = along // (CHIPS_Z - 1) * (1 - fold)
    far = (CHIPS_Z - 1 - along) // (CHIPS_Z - 1) * has_south
    near = has_south - far
    relay_north = ((along == CHIPS_Z - 2) & (a >= CHIPS_Z)).astype(jnp.int32)
    relay_south = ((along == 1) & (a < n_lat - CHIPS_Z)).astype(jnp.int32)
    north_lon = s + fold * (n_lon - 1 - 2 * s)
    north_lat = a + 1 - fold
    east = lax.rem(s + 1, n_lon)
    west = lax.rem(s + n_lon - 1, n_lon)
    groups = ROWS // GROUP
    top = GROUP + ROWS
    lane = lanes()
    fields = (forcing, kappa_lon, kappa_lat, shear, amplitude)

    def load(g, i, q, sem):
        cells = pl.ds(q * WIDTH, WIDTH)
        return pltpu.make_async_copy(fields[i].at[:, pl.ds(g * GROUP, GROUP), cells], raw.at[g, i, q], sem)

    def load_group(g):
        for i in range(4):
            for q in range(TILES):
                load(g, i, q, load_sem.at[g]).start()

    owner_copy = pltpu.make_async_copy(owner, owner_s, owner_sem.at[0])
    owner_copy_v = pltpu.make_async_copy(owner, owner_v, owner_sem.at[1])
    load_group(groups - 1)
    owner_copy.start()

    barrier = pltpu.get_barrier_semaphore()

    def enter(condition, lon, lat):
        @pl.when(condition == 1)
        def _():
            pl.semaphore_signal(barrier, inc=1, device_id=(lon, lat), device_id_type=MESH)

    enter(1 - fold - wrap, s, a + 1)
    enter(has_south, s, a - 1)
    enter(far, s, a + CHIPS_Z - 2)
    enter(relay_north, s, a - (CHIPS_Z - 1))
    enter(relay_south, s, a + CHIPS_Z - 1)
    enter(relay_south, s, a + CHIPS_Z - 2)
    for d in range(1, OWNERS):
        pl.semaphore_signal(barrier, inc=1, device_id=(lax.rem(s + d, n_lon), a), device_id_type=MESH)

    load_group(0)
    load_group(1)
    owner_copy_v.start()
    for g in range(groups):
        for q in range(TILES):
            load(g, 4, q, load_sem.at[groups]).start()

    flat = raw.reshape(groups * 5 * TILES * LEVELS * GROUP, WIDTH)

    def cells_of(g, i, q, rr):
        return flat[pl.ds(((g * 5 + i) * TILES + q) * LEVELS * GROUP + rr, LEVELS, GROUP)]

    def prepare_group(g):
        whole = raw.at[g, pl.ds(0, 4)]
        pltpu.make_async_copy(whole, whole, load_sem.at[g]).wait()

        def prepare(rr, _):
            r = g * GROUP + rr
            for q in range(TILES):
                sea = (owner_s[r, q] >= 0).astype(jnp.float32)
                k_lon = cells_of(g, 1, q, rr)
                k_lat = cells_of(g, 2, q, rr)
                cross = 0.5 * cells_of(g, 3, q, rr) * jnp.sqrt(k_lon * k_lat)
                field[GROUP + r, 0, q] = sea * cells_of(g, 0, q, rr)
                field[GROUP + r, 1, q] = sea * k_lon
                field[GROUP + r, 2, q] = sea * k_lat
                field[GROUP + r, 3, q] = sea * cross
            return 0

        lax.fori_loop(0, GROUP, prepare, 0)

    def remote(src, dst, ssem, rsem, lon, lat):
        return pltpu.make_async_remote_copy(
            src_ref=src, dst_ref=dst, send_sem=ssem, recv_sem=rsem, device_id=(lon, lat), device_id_type=MESH
        )

    def part(ref, place, k, first=0, count=TILES):
        return ref.at[place, pl.ds(0, 4 if k < ITERS else 1), pl.ds(first, count)]

    half = TILES // 2

    def north_copies(k_size, k):
        own = top - k
        plain = remote(
            part(field, own, k_size), part(field, GROUP - k + fold * (top - 1 - GROUP + 2 * k), k_size),
            north_ssem.at[k - 1], lat_rsem.at[fold, 0, k - 1], north_lon, north_lat,
        )
        direct = remote(
            part(field, own, k_size, 0, half), part(field, GROUP - k, k_size, 0, half),
            north_ssem.at[k - 1], lat_rsem.at[0, 0, k - 1], s, north_lat,
        )
        around = remote(
            part(field, own, k_size, half, half), part(stage, k - 1, k_size, half, half),
            relay_ssem.at[k - 1], stage_rsem.at[k - 1], s, lax.rem(a + CHIPS_Z - 1, n_lat),
        )
        return plain, direct, around

    def south_copies(k_size, k):
        own = GROUP + k - 1
        plain = remote(
            part(field, own, k_size), part(field, top + k - 1, k_size),
            south_ssem.at[k - 1], lat_rsem.at[1, 0, k - 1], s, lax.rem(a + n_lat - 1, n_lat),
        )
        around = remote(
            part(field, own, k_size), part(stage, k - 1, k_size),
            south_ssem.at[k - 1], stage_rsem.at[k - 1], s, lax.rem(a + n_lat - (CHIPS_Z - 1), n_lat),
        )
        return plain, around

    def each_row(low, high, act):
        for_size = min(high, ITERS - 1)

        def one(k, _):
            act(1, k)
            return 0

        lax.fori_loop(low, for_size + 1, one, 0)
        if high == ITERS:
            act(ITERS, ITERS)

    def send_north(low, high):
        def act(k_size, k):
            plain, direct, around = north_copies(k_size, k)

            @pl.when(wrap == 0)
            def _():
                plain.start()

            @pl.when(wrap == 1)
            def _():
                direct.start()
                around.start()

        each_row(low, high, act)

    def send_south(low, high):
        def act(k_size, k):
            plain, around = south_copies(k_size, k)

            @pl.when(near == 1)
            def _():
                plain.start()

            @pl.when(far == 1)
            def _():
                around.start()

        each_row(low, high, act)

    ends_north = remote(
        lon_recv.at[groups - 1], lat_recv.at[fold], ends_ssem.at[0], ends_rsem.at[fold], north_lon, north_lat
    )
    ends_south = remote(
        lon_recv.at[0], lat_recv.at[1], ends_ssem.at[1], ends_rsem.at[1], s, lax.rem(a + n_lat - 1, n_lat)
    )
    ends_around = remote(
        lon_recv.at[0], stage_ends, ends_ssem.at[1], ends_rsem.at[2], s, lax.rem(a + n_lat - (CHIPS_Z - 1), n_lat)
    )
    ends_forward = remote(stage_ends, lat_recv.at[1], ends_ssem.at[2], ends_rsem.at[1], s, lax.rem(a + CHIPS_Z - 2, n_lat))
    to_west = remote(lon_send.at[0], lon_recv.at[:, 0], lon_ssem.at[0], lon_rsem.at[0], west, a)
    to_east = remote(lon_send.at[1], lon_recv.at[:, 1], lon_ssem.at[1], lon_rsem.at[1], east, a)
    early = ITERS // 2

    owner_copy.wait()
    prepare_group(groups - 1)
    pl.semaphore_wait(barrier, OWNERS - 1 + (1 - fold) + near + 2 * wrap + far + relay_north)

    @pl.when(wrap == 1)
    def _():
        pl.semaphore_signal(ready_sem, inc=1, device_id=(s, a - (CHIPS_Z - 2)), device_id_type=MESH)

    @pl.when(fold == 0)
    def _():
        send_north(1, early)

    prepare_group(0)

    @pl.when(has_south == 1)
    def _():
        send_south(1, early)

    prepare_group(1)

    per_vector = WIDTH // GROUP

    def pack_group(g, _):
        for v in range(PIECES):
            to_west_v = jnp.zeros((LEVELS, WIDTH), jnp.float32)
            to_east_v = jnp.zeros((LEVELS, WIDTH), jnp.float32)
            for j in range(per_vector):
                rr, kind = divmod(v * per_vector + j, 4)
                r = GROUP + g * GROUP + rr
                here = lane // GROUP == j
                first, last = field[r, kind, 0], field[r, kind, TILES - 1]
                if j:
                    first = pltpu.roll(first, GROUP * j, axis=1)
                if j < per_vector - 1:
                    last = pltpu.roll(last, GROUP * (j + 1), axis=1)
                to_west_v = jnp.where(here, first, to_west_v)
                to_east_v = jnp.where(here, last, to_east_v)
            lon_send[0, g, v] = to_west_v
            lon_send[1, g, v] = to_east_v
        return 0

    lax.fori_loop(0, groups, pack_group, 0)
    to_west.start()
    to_east.start()

    @pl.when(fold == 1)
    def _():
        send_north(1, early)

    def unpack(buf, g, base, step):
        for v in range(PIECES):
            from_east, from_west = buf[g, 0, v], buf[g, 1, v]
            for j in range(per_vector):
                rr, kind = divmod(v * per_vector + j, 4)
                after = from_east if j == 0 else pltpu.roll(from_east, WIDTH - GROUP * j, axis=1)
                before = from_west if j == per_vector - 1 else pltpu.roll(from_west, WIDTH - GROUP * (j + 1), axis=1)
                ends = jnp.where(lane < ITERS, after, jnp.where(lane >= WIDTH - ITERS, before, 0.0))
                field[base + step * rr, kind, TILES] = ends

    amplitudes = raw.at[:, pl.ds(4, 1)]
    pltpu.make_async_copy(amplitudes, amplitudes, load_sem.at[groups]).wait()

    def scale_group(g, _):
        def scale_row(rr, _):
            for q in range(TILES):
                scale[g * GROUP + rr, q] = cells_of(g, 4, q, rr)
            return 0

        return lax.fori_loop(0, GROUP, scale_row, 0)

    lax.fori_loop(0, groups, scale_group, 0)

    owner_copy_v.wait()
    down = lax.broadcasted_iota(jnp.int32, (LEVELS, WIDTH), 0)
    column = lax.rem(lane, TILES)
    carried = jnp.zeros((1, WIDTH), jnp.int32)
    ranks, numbers = [], []
    for g in range(groups):
        rows = owner_v[pl.ds(g * GROUP, GROUP), :]
        spread = jnp.broadcast_to(rows[:, 0:1], (GROUP, WIDTH))
        for q in range(1, TILES):
            spread = jnp.where(column == q, jnp.broadcast_to(rows[:, q : q + 1], (GROUP, WIDTH)), spread)
        mine = (spread == lane // TILES).astype(jnp.int32)
        within = mine + jnp.where(column >= 1, pltpu.roll(mine, 1, axis=1), 0)
        within = within + jnp.where(column >= 2, pltpu.roll(within, 2, axis=1), 0)
        total = mine + jnp.where(column % 2 == 0, pltpu.roll(mine, WIDTH - 1, axis=1), pltpu.roll(mine, 1, axis=1))
        total = total + jnp.where(column < 2, pltpu.roll(total, WIDTH - 2, axis=1), pltpu.roll(total, 2, axis=1))
        upto = total
        for shift in (1, 2, 4):
            upto = upto + jnp.where(down >= shift, pltpu.roll(upto, shift, axis=0), 0)
        ranks.append(jnp.where(mine == 1, carried + upto - total + within, 0))
        numbers.append((g * GROUP + down) * TILES + column + 1)
        carried = carried + jnp.sum(total, axis=0, keepdims=True)
    for k in range(MOST):
        place = jnp.zeros((LEVELS, WIDTH), jnp.int32)
        for g in range(groups):
            place = place + jnp.where(ranks[g] == k + 1, numbers[g], 0)
        place = jnp.sum(place, axis=0, keepdims=True)
        place = place + pltpu.roll(jnp.broadcast_to(place, (LEVELS, WIDTH)), WIDTH - 1, axis=1)
        place = place + pltpu.roll(place, WIDTH - 2, axis=1)
        index_v[k : k + 1, :] = place[0:1, :] - 1
    index_copy = pltpu.make_async_copy(index_v, index_s, index_sem)
    index_copy.start()

    to_west.wait_recv()
    to_east.wait_recv()
    ends_north.start()
    send_north(early + 1, ITERS)

    @pl.when(near == 1)
    def _():
        ends_south.start()

    @pl.when(far == 1)
    def _():
        ends_around.start()

    @pl.when(has_south == 1)
    def _():
        send_south(early + 1, ITERS)

    def unpack_own(g, _):
        unpack(lon_recv, g, GROUP + g * GROUP, 1)
        return 0

    lax.fori_loop(0, groups, unpack_own, 0)

    def relay_copies(k_size, k):
        north = remote(
            part(stage, k - 1, k_size, half, half), part(field, GROUP - k, k_size, half, half),
            forward_ssem.at[k - 1], lat_rsem.at[0, 1, k - 1], s, lax.rem(a + n_lat - (CHIPS_Z - 2), n_lat),
        )
        south = remote(
            part(stage, k - 1, k_size), part(field, top + k - 1, k_size),
            forward_ssem.at[k - 1], lat_rsem.at[1, 0, k - 1], s, lax.rem(a + CHIPS_Z - 2, n_lat),
        )
        return north, south

    for turn in range(1, ITERS + 1):
        sweep(field, later, turn, GROUP + turn, ROWS - 2 * turn)

        @pl.when(relay_north == 1)
        def _():
            north_copies(turn, turn)[2].wait_recv()
            relay_copies(turn, turn)[0].start()

    def clear(r, _):
        zero = jnp.zeros((LEVELS, WIDTH), jnp.float32)
        for kind in range(4):
            for q in range(RING):
                field[r, kind, q] = zero
        return 0

    def mirrored(value):
        return jnp.take_along_axis(value, WIDTH - 1 - lane, axis=1)

    def mirror_ends(i, _):
        for kind in range(4):
            field[top + i, kind, TILES] = mirrored(field[top + i, kind, TILES])
        return 0

    def mirror_row(r):
        for kind in range(4):
            old = [field[r, kind, q] for q in range(TILES)]
            for q in range(TILES):
                field[r, kind, q] = mirrored(old[TILES - 1 - q])

    late = wrap + fold

    def edge(i, _):
        side = lax.rem(i + 1 - late, 2)
        step = 1 - 2 * side
        sign = step.astype(jnp.float32)
        arrives = (side + has_south + 1) // 2
        mirror = side * fold
        halves = (1 - side) * far

        @pl.when(arrives == 1)
        def _():
            remote(
                lon_recv.at[0], lat_recv.at[side], ends_ssem.at[0], ends_rsem.at[side], north_lon, north_lat
            ).wait_recv()
            unpack(lat_recv, side, side * top + mirror * (GROUP - 1), 1 - 2 * mirror)

        @pl.when(mirror == 1)
        def _():
            lax.fori_loop(0, GROUP, mirror_ends, 0)

        @pl.when(arrives == 0)
        def _():
            lax.fori_loop(0, GROUP, clear, 0)

        def arrive(k_size, k):
            def await_row(part_of, first, count):
                place = part(field, GROUP, k_size, first, count)
                remote(
                    place, place, north_ssem.at[k - 1], lat_rsem.at[side, part_of, k - 1], north_lon, north_lat
                ).wait_recv()

            @pl.when(arrives - halves == 1)
            def _():
                await_row(0, 0, TILES)

            @pl.when(halves == 1)
            def _():
                await_row(0, 0, half)
                await_row(1, half, half)

            @pl.when(mirror == 1)
            def _():
                mirror_row(top + k - 1)

        def outward(k, _):
            @pl.when(k < ITERS)
            def _():
                arrive(1, k)

            @pl.when(k == ITERS)
            def _():
                arrive(ITERS, ITERS)

            diagonal(field, later, GROUP + side * (ROWS - 1) + step * (1 - k), step, sign)
            return 0

        lax.fori_loop(1, ITERS + 1, outward, 0)
        return 0

    lax.fori_loop(0, 2, edge, 0)

    @pl.when(relay_south == 1)
    def _():
        pl.semaphore_wait(ready_sem, 1)
        ends_around.wait_recv()
        ends_forward.start()

        def act(k_size, k):
            south_copies(k_size, k)[1].wait_recv()
            relay_copies(k_size, k)[1].start()

        each_row(1, ITERS, act)

    index_copy.wait()

    def fill(o):
        for k in range(MOST):
            t = index_s[k, o * TILES]
            r = jnp.maximum(t, 0) // TILES
            q = jnp.maximum(t, 0) - r * TILES
            tile = scale[r, q] * later[(ITERS - 1) % 2, GROUP + r, q]
            packed[o * MOST + k] = jnp.where(t >= 0, tile, 0.0)

    def to_owner(o, d):
        block = pl.ds(o * MOST, MOST)
        slot = pl.ds(s * MOST, MOST)
        return remote(packed.at[block], out.at[0, slot], out_ssem.at[d], out_rsem.at[d], o, a)

    def give(d, _):
        o = lax.rem(s + d, n_lon)
        fill(o)
        to_owner(o, d).start()
        return 0

    lax.fori_loop(1, OWNERS, give, 0)
    fill(s)
    own = pltpu.make_async_copy(packed.at[pl.ds(s * MOST, MOST)], out.at[0, pl.ds(s * MOST, MOST)], own_sem)
    own.start()
    to_west.wait_send()
    to_east.wait_send()
    ends_north.wait_send()

    def drain(k_size, k):
        plain, direct, around = north_copies(k_size, k)

        @pl.when(wrap == 0)
        def _():
            plain.wait_send()

        @pl.when(wrap == 1)
        def _():
            direct.wait_send()
            around.wait_send()

        @pl.when(has_south == 1)
        def _():
            south_copies(k_size, k)[0].wait_send()

        @pl.when(relay_north == 1)
        def _():
            relay_copies(k_size, k)[0].wait_send()

        @pl.when(relay_south == 1)
        def _():
            relay_copies(k_size, k)[1].wait_send()

    each_row(1, ITERS, drain)

    @pl.when(has_south == 1)
    def _():
        ends_south.wait_send()

    @pl.when(relay_south == 1)
    def _():
        ends_forward.wait_send()

    own.wait()

    def finish(d, _):
        to_owner(lax.rem(s + d, n_lon), d).wait()
        return 0

    lax.fori_loop(1, OWNERS, finish, 0)


def per_device(forcing, kappa_lon, kappa_lat, shear, amplitude, tile_owner):
    vmem = functools.partial(pltpu.VMEM, dtype=jnp.float32)
    dma = pltpu.SemaphoreType.DMA
    return pl.pallas_call(
        kernel,
        out_shape=jax.ShapeDtypeStruct((1, OWNERS * MOST, LEVELS, WIDTH), jnp.float32),
        in_specs=[pl.BlockSpec(memory_space=pl.ANY)] * 6,
        out_specs=pl.BlockSpec(memory_space=pl.ANY),
        scratch_shapes=[
            vmem((ROWS // GROUP, 5, TILES, LEVELS, GROUP, WIDTH)),
            vmem((TOTAL, 4, RING, LEVELS, WIDTH)),
            vmem((2, TOTAL, RING, LEVELS, WIDTH)),
            vmem((ROWS, TILES, LEVELS, WIDTH)),
            vmem((ITERS, 4, TILES, LEVELS, WIDTH)),
            vmem((2, PIECES, LEVELS, WIDTH)),
            vmem((2, ROWS // GROUP, PIECES, LEVELS, WIDTH)),
            vmem((ROWS // GROUP, 2, PIECES, LEVELS, WIDTH)),
            vmem((2, 2, PIECES, LEVELS, WIDTH)),
            vmem((OWNERS * MOST, LEVELS, WIDTH)),
            pltpu.SMEM((ROWS, TILES), jnp.int32),
            pltpu.VMEM((ROWS, TILES), jnp.int32),
            pltpu.VMEM((2 * LEVELS, WIDTH), jnp.int32),
            pltpu.SMEM((2 * LEVELS, WIDTH), jnp.int32),
            dma((ROWS // GROUP + 1,)),
            dma((2,)),
            pltpu.SemaphoreType.REGULAR,
            dma((2,)),
            dma((2,)),
            dma((ITERS,)),
            dma((ITERS,)),
            dma((ITERS,)),
            dma((2, 2, ITERS)),
            dma((3,)),
            dma((3,)),
            dma((ITERS,)),
            dma((ITERS,)),
            dma((OWNERS,)),
            dma((OWNERS,)),
            dma,
            dma,
        ],
        compiler_params=pltpu.CompilerParams(collective_id=0, has_side_effects=True),
    )(forcing, kappa_lon, kappa_lat, shear, amplitude, tile_owner)


def solution(mesh):
    return jax.shard_map(
        per_device,
        mesh=mesh,
        in_specs=(P(None, "lat", "lon"),) * 5 + (P("lat", "lon"),),
        out_specs=P("lat", "lon", None, None),
        check_vma=False,
    )
```

time: 65.3 us -> 46.3 us (0.71)
  the two profiles are of different devices: /device:TPU:29 before, /device:TPU:6 now
where the time goes in v2:
time: 46.3 us; the launch traced here: 45.4 us
  Pallas kernels  42.3 us (91%)
  local copies, waits for them, and re-layouts  3.13 us (7%)
    pallas_call x1, Pallas kernels, per_device(): pl.pallas_call(kernel, out_shape=jax.ShapeDtypeStruct((1, OWNERS * MOST,...  42.3 us
    unnamed x2, local copies, waits for them, and re-layouts  3.13 us

profile of v2, /device:TPU:6, one launch (start us, length us, event | category | flops | bytes accessed | tf_op | source)
XLA Modules:
  0.0 45.4 jit_solution(4215755954611245802)
XLA Ops:
  0.0 1.4 %copy.7.owner = s32[24,4]{1,0:T(8,128)} copy(s32[24,4]{0,1:T(4,128)} %param.11) | data formatting | bytes 768 | tf_op args[5]
  1.4 42.3 %shard_map.64 = f32[1,96,8,128]{3,2,1,0:T(8,128)} custom-call(f32[8,24,512]{2,1,0:T(8,128)} %forcing.1, f32[8,24,512]{2,1,0:T(8,128)} %kappa_lon.1, f32[8,24,512]{2,1,0:T(8,128)} %kappa_lat.1, f32[8,24,512]{2,1,0:T(8,128)} %shear.1, f32[8,24,512]{2,1,0:T(8,128)} %amplitude.1, s32[24,4]{1,0:T(8,128)} %copy.7.owner), custom_call_target="tpu_custom_call" | custom-call | tf_op jit(solution)/shard_map/pallas_call | solution.py:589
  43.7 1.8 %copy.9 = f32[1,96,8,128]{3,2,1,0:T(8,128)} copy(f32[1,96,8,128]{3,2,1,0:T(8,128)} %shard_map.64) | data formatting | bytes 786432

commit v3 on v2

--- a/solution.py
+++ b/solution.py
@@ -8,6 +8,8 @@
 from jax.sharding import PartitionSpec as P
 
 ITERS = 6
+RELAYED = 6
+DEEP = ITERS // 2
 LEVELS = 8
 WIDTH = 128
 ROWS = 24
@@ -76,23 +78,25 @@
     lax.fori_loop(0, count, body, (south, south_slope, centre, both, slope), unroll=2)
 
 
-def diagonal(field, later, start, step, sign):
+def wedge(field, later, start, step, sign):
     lane = lanes()
-    outer = row_of(field, later, 0, start - step)
+    rows = [row_of(field, later, 0, start + step * (j - 1)) for j in range(DEEP)]
     for turn in range(1, ITERS + 1):
-        r = start + step * (turn - 1)
-        centre = row_of(field, later, turn - 1, r)
-        inner = row_of(field, later, turn - 1, r + step)
-        both, _ = neighbours(centre, lane)
-        _, inner_slope = neighbours(inner, lane)
-        _, outer_slope = neighbours(outer, lane)
-        outer = updated(field, r, outer, centre, inner, (outer_slope, both, inner_slope), sign)
-        store(later, turn, r, outer)
+        base = start + step * (turn - 1)
+        rows = rows + [row_of(field, later, turn - 1, base + step * (DEEP - 1 + j)) for j in range(2)]
+        terms = [neighbours(row, lane) for row in rows]
+        new = []
+        for j in range(DEEP):
+            around = (terms[j][1], terms[j + 1][0], terms[j + 2][1])
+            new.append(updated(field, base + step * j, rows[j], rows[j + 1], rows[j + 2], around, sign))
+        for j in range(DEEP):
+            store(later, turn, base + step * j, new[j])
+        rows = new
 
 
 def kernel(
     forcing, kappa_lon, kappa_lat, shear, amplitude, owner, out,
-    raw, field, later, scale, stage, stage_ends, lon_send, lon_recv, lat_recv, packed, owner_s, owner_v, index_v, index_s,
+    raw, field, later, scale, stage, lon_send, lon_recv, lat_recv, packed, owner_s, index_v, index_s,
     load_sem, owner_sem, ready_sem, lon_ssem, lon_rsem, north_ssem, relay_ssem, south_ssem, lat_rsem,
     ends_ssem, ends_rsem, stage_rsem, forward_ssem, out_ssem, out_rsem, own_sem, index_sem,
 ):
@@ -107,6 +111,7 @@
     far = (CHIPS_Z - 1 - along) // (CHIPS_Z - 1) * has_south
     near = has_south - far
     relay_north = ((along == CHIPS_Z - 2) & (a >= CHIPS_Z)).astype(jnp.int32)
+    yields = (a == n_lat - CHIPS_Z).astype(jnp.int32)
     relay_south = ((along == 1) & (a < n_lat - CHIPS_Z)).astype(jnp.int32)
     north_lon = s + fold * (n_lon - 1 - 2 * s)
     north_lat = a + 1 - fold
@@ -127,7 +132,6 @@
                 load(g, i, q, load_sem.at[g]).start()
 
     owner_copy = pltpu.make_async_copy(owner, owner_s, owner_sem.at[0])
-    owner_copy_v = pltpu.make_async_copy(owner, owner_v, owner_sem.at[1])
     load_group(groups - 1)
     owner_copy.start()
 
@@ -138,21 +142,17 @@
         def _():
             pl.semaphore_signal(barrier, inc=1, device_id=(lon, lat), device_id_type=MESH)
 
-    enter(1 - fold - wrap, s, a + 1)
-    enter(has_south, s, a - 1)
+    for side_lon in (west, s, east):
+        enter(1 - fold - wrap, side_lon, a + 1)
+        enter(has_south, side_lon, a - 1)
     enter(far, s, a + CHIPS_Z - 2)
-    enter(relay_north, s, a - (CHIPS_Z - 1))
     enter(relay_south, s, a + CHIPS_Z - 1)
     enter(relay_south, s, a + CHIPS_Z - 2)
+    enter(relay_north, s, a - (CHIPS_Z - 1))
     for d in range(1, OWNERS):
         pl.semaphore_signal(barrier, inc=1, device_id=(lax.rem(s + d, n_lon), a), device_id_type=MESH)
 
     load_group(0)
-    load_group(1)
-    owner_copy_v.start()
-    for g in range(groups):
-        for q in range(TILES):
-            load(g, 4, q, load_sem.at[groups]).start()
 
     flat = raw.reshape(groups * 5 * TILES * LEVELS * GROUP, WIDTH)
 
@@ -166,7 +166,7 @@
         def prepare(rr, _):
             r = g * GROUP + rr
             for q in range(TILES):
-                sea = (owner_s[r, q] >= 0).astype(jnp.float32)
+                sea = (owner_s[q, r] >= 0).astype(jnp.float32)
                 k_lon = cells_of(g, 1, q, rr)
                 k_lat = cells_of(g, 2, q, rr)
                 cross = 0.5 * cells_of(g, 3, q, rr) * jnp.sqrt(k_lon * k_lat)
@@ -210,11 +210,15 @@
             part(field, own, k_size), part(field, top + k - 1, k_size),
             south_ssem.at[k - 1], lat_rsem.at[1, 0, k - 1], s, lax.rem(a + n_lat - 1, n_lat),
         )
+        direct = remote(
+            part(field, own, k_size, 0, half), part(field, top + k - 1, k_size, 0, half),
+            south_ssem.at[k - 1], lat_rsem.at[1, 0, k - 1], s, lax.rem(a + n_lat - 1, n_lat),
+        )
         around = remote(
-            part(field, own, k_size), part(stage, k - 1, k_size),
-            south_ssem.at[k - 1], stage_rsem.at[k - 1], s, lax.rem(a + n_lat - (CHIPS_Z - 1), n_lat),
-        )
-        return plain, around
+            part(field, own, k_size, half, half), part(stage, k - 1, k_size, half, half),
+            relay_ssem.at[k - 1], stage_rsem.at[k - 1], s, lax.rem(a + n_lat - (CHIPS_Z - 1), n_lat),
+        )
+        return plain, direct, around
 
     def each_row(low, high, act):
         for_size = min(high, ITERS - 1)
@@ -230,69 +234,54 @@
     def send_north(low, high):
         def act(k_size, k):
             plain, direct, around = north_copies(k_size, k)
-
-            @pl.when(wrap == 0)
+            split = (wrap == 1) & (k <= RELAYED)
+
+            @pl.when(~split)
             def _():
                 plain.start()
 
-            @pl.when(wrap == 1)
+            @pl.when(split)
             def _():
                 direct.start()
                 around.start()
 
         each_row(low, high, act)
 
-    def send_south(low, high):
-        def act(k_size, k):
-            plain, around = south_copies(k_size, k)
-
-            @pl.when(near == 1)
-            def _():
-                plain.start()
-
-            @pl.when(far == 1)
-            def _():
-                around.start()
-
-        each_row(low, high, act)
-
-    ends_north = remote(
-        lon_recv.at[groups - 1], lat_recv.at[fold], ends_ssem.at[0], ends_rsem.at[fold], north_lon, north_lat
+    def send_south(near_or_far):
+        for j in range(2):
+            ends_copy("south", j).start()
+        each_row(1, ITERS, lambda k_size, k: south_copies(k_size, k)[near_or_far].start())
+
+    ends_mirrored = remote(
+        lon_recv.at[groups - 1], lat_recv.at[1], ends_ssem.at[0, 0], ends_rsem.at[1, 0], north_lon, north_lat
     )
-    ends_south = remote(
-        lon_recv.at[0], lat_recv.at[1], ends_ssem.at[1], ends_rsem.at[1], s, lax.rem(a + n_lat - 1, n_lat)
-    )
-    ends_around = remote(
-        lon_recv.at[0], stage_ends, ends_ssem.at[1], ends_rsem.at[2], s, lax.rem(a + n_lat - (CHIPS_Z - 1), n_lat)
-    )
-    ends_forward = remote(stage_ends, lat_recv.at[1], ends_ssem.at[2], ends_rsem.at[1], s, lax.rem(a + CHIPS_Z - 2, n_lat))
+    south_lat = lax.rem(a + n_lat - 1, n_lat)
+
+    def ends_copy(kind, j):
+        lon = (west, east)[j]
+        if kind == "north":
+            return remote(
+                lon_send.at[j, groups - 1], lat_recv.at[0, j], ends_ssem.at[0, j], ends_rsem.at[0, j], lon, north_lat
+            )
+        return remote(lon_send.at[j, 0], lat_recv.at[1, j], ends_ssem.at[1, j], ends_rsem.at[1, j], lon, south_lat)
+
     to_west = remote(lon_send.at[0], lon_recv.at[:, 0], lon_ssem.at[0], lon_rsem.at[0], west, a)
     to_east = remote(lon_send.at[1], lon_recv.at[:, 1], lon_ssem.at[1], lon_rsem.at[1], east, a)
-    early = ITERS // 2
+    early = 4
 
     owner_copy.wait()
     prepare_group(groups - 1)
-    pl.semaphore_wait(barrier, OWNERS - 1 + (1 - fold) + near + 2 * wrap + far + relay_north)
+    pl.semaphore_wait(barrier, OWNERS - 1 + 3 * (1 - fold) + 3 * near + 2 * wrap + far + relay_north)
 
     @pl.when(wrap == 1)
     def _():
+        for side_lon in (west, s, east):
+            pl.semaphore_signal(ready_sem, inc=1, device_id=(side_lon, a + 1), device_id_type=MESH)
         pl.semaphore_signal(ready_sem, inc=1, device_id=(s, a - (CHIPS_Z - 2)), device_id_type=MESH)
 
-    @pl.when(fold == 0)
-    def _():
-        send_north(1, early)
-
-    prepare_group(0)
-
-    @pl.when(has_south == 1)
-    def _():
-        send_south(1, early)
-
-    prepare_group(1)
-
     per_vector = WIDTH // GROUP
 
-    def pack_group(g, _):
+    def pack_group(g):
         for v in range(PIECES):
             to_west_v = jnp.zeros((LEVELS, WIDTH), jnp.float32)
             to_east_v = jnp.zeros((LEVELS, WIDTH), jnp.float32)
@@ -309,15 +298,44 @@
                 to_east_v = jnp.where(here, last, to_east_v)
             lon_send[0, g, v] = to_west_v
             lon_send[1, g, v] = to_east_v
-        return 0
-
-    lax.fori_loop(0, groups, pack_group, 0)
+
+    @pl.when(fold == 0)
+    def _():
+        send_north(1, early)
+
+    pack_group(groups - 1)
+
+    @pl.when(fold == 0)
+    def _():
+        for j in range(2):
+            ends_copy("north", j).start()
+
+    load_group(1)
+    prepare_group(0)
+    pack_group(0)
+    for g in range(groups):
+        for q in range(TILES):
+            load(g, 4, q, load_sem.at[groups]).start()
+    prepare_group(1)
+    pack_group(1)
     to_west.start()
     to_east.start()
 
+    @pl.when(fold == 0)
+    def _():
+        send_north(early + 1, ITERS)
+
     @pl.when(fold == 1)
     def _():
-        send_north(1, early)
+        send_north(1, ITERS)
+
+    @pl.when(near == 1)
+    def _():
+        send_south(0)
+
+    @pl.when(far == 1)
+    def _():
+        each_row(1, ITERS, lambda k_size, k: south_copies(k_size, k)[2].start())
 
     def unpack(buf, g, base, step):
         for v in range(PIECES):
@@ -342,16 +360,15 @@
 
     lax.fori_loop(0, groups, scale_group, 0)
 
-    owner_copy_v.wait()
     down = lax.broadcasted_iota(jnp.int32, (LEVELS, WIDTH), 0)
     column = lax.rem(lane, TILES)
     carried = jnp.zeros((1, WIDTH), jnp.int32)
     ranks, numbers = [], []
     for g in range(groups):
-        rows = owner_v[pl.ds(g * GROUP, GROUP), :]
-        spread = jnp.broadcast_to(rows[:, 0:1], (GROUP, WIDTH))
-        for q in range(1, TILES):
-            spread = jnp.where(column == q, jnp.broadcast_to(rows[:, q : q + 1], (GROUP, WIDTH)), spread)
+        spread = jnp.full((GROUP, WIDTH), -1, jnp.int32)
+        for rr in range(GROUP):
+            for q in range(TILES):
+                spread = jnp.where((down == rr) & (column == q), owner_s[q, g * GROUP + rr], spread)
         mine = (spread == lane // TILES).astype(jnp.int32)
         within = mine + jnp.where(column >= 1, pltpu.roll(mine, 1, axis=1), 0)
         within = within + jnp.where(column >= 2, pltpu.roll(within, 2, axis=1), 0)
@@ -376,20 +393,10 @@
 
     to_west.wait_recv()
     to_east.wait_recv()
-    ends_north.start()
-    send_north(early + 1, ITERS)
-
-    @pl.when(near == 1)
-    def _():
-        ends_south.start()
-
-    @pl.when(far == 1)
-    def _():
-        ends_around.start()
-
-    @pl.when(has_south == 1)
-    def _():
-        send_south(early + 1, ITERS)
+
+    @pl.when(fold == 1)
+    def _():
+        ends_mirrored.start()
 
     def unpack_own(g, _):
         unpack(lon_recv, g, GROUP + g * GROUP, 1)
@@ -403,8 +410,8 @@
             forward_ssem.at[k - 1], lat_rsem.at[0, 1, k - 1], s, lax.rem(a + n_lat - (CHIPS_Z - 2), n_lat),
         )
         south = remote(
-            part(stage, k - 1, k_size), part(field, top + k - 1, k_size),
-            forward_ssem.at[k - 1], lat_rsem.at[1, 0, k - 1], s, lax.rem(a + CHIPS_Z - 2, n_lat),
+            part(stage, k - 1, k_size, half, half), part(field, top + k - 1, k_size, half, half),
+            forward_ssem.at[k - 1], lat_rsem.at[1, 1, k - 1], s, lax.rem(a + CHIPS_Z - 2, n_lat),
         )
         return north, south
 
@@ -447,11 +454,26 @@
         mirror = side * fold
         halves = (1 - side) * far
 
+        @pl.when(halves - yields == 1)
+        def _():
+            pl.semaphore_wait(ready_sem, 3)
+            send_south(1)
+
+        whole = side * fold
+
+        @pl.when(whole == 1)
+        def _():
+            remote(lon_recv.at[0], lat_recv.at[side], ends_ssem.at[0, 0], ends_rsem.at[side, 0], s, south_lat).wait_recv()
+
+        @pl.when(arrives - whole == 1)
+        def _():
+            for j in range(2):
+                remote(
+                    lon_send.at[j, 0], lat_recv.at[side, j], ends_ssem.at[0, j], ends_rsem.at[side, j], s, south_lat
+                ).wait_recv()
+
         @pl.when(arrives == 1)
         def _():
-            remote(
-                lon_recv.at[0], lat_recv.at[side], ends_ssem.at[0], ends_rsem.at[side], north_lon, north_lat
-            ).wait_recv()
             unpack(lat_recv, side, side * top + mirror * (GROUP - 1), 1 - 2 * mirror)
 
         @pl.when(mirror == 1)
@@ -469,11 +491,13 @@
                     place, place, north_ssem.at[k - 1], lat_rsem.at[side, part_of, k - 1], north_lon, north_lat
                 ).wait_recv()
 
-            @pl.when(arrives - halves == 1)
+            split = ((halves == 1) & (k <= RELAYED)) | (side * wrap == 1)
+
+            @pl.when((arrives == 1) & ~split)
             def _():
                 await_row(0, 0, TILES)
 
-            @pl.when(halves == 1)
+            @pl.when(split)
             def _():
                 await_row(0, 0, half)
                 await_row(1, half, half)
@@ -482,34 +506,28 @@
             def _():
                 mirror_row(top + k - 1)
 
-        def outward(k, _):
-            @pl.when(k < ITERS)
+        def outward(h, _):
+            def one(j, _):
+                arrive(1, h * DEEP + j)
+                return 0
+
+            lax.fori_loop(1, DEEP, one, 0)
+
+            @pl.when(h == 0)
             def _():
-                arrive(1, k)
-
-            @pl.when(k == ITERS)
+                arrive(1, DEEP)
+
+            @pl.when(h == 1)
             def _():
                 arrive(ITERS, ITERS)
 
-            diagonal(field, later, GROUP + side * (ROWS - 1) + step * (1 - k), step, sign)
+            wedge(field, later, GROUP + side * (ROWS - 1) + step * (1 - DEEP * (h + 1)), step, sign)
             return 0
 
-        lax.fori_loop(1, ITERS + 1, outward, 0)
+        lax.fori_loop(0, 2, outward, 0)
         return 0
 
     lax.fori_loop(0, 2, edge, 0)
-
-    @pl.when(relay_south == 1)
-    def _():
-        pl.semaphore_wait(ready_sem, 1)
-        ends_around.wait_recv()
-        ends_forward.start()
-
-        def act(k_size, k):
-            south_copies(k_size, k)[1].wait_recv()
-            relay_copies(k_size, k)[1].start()
-
-        each_row(1, ITERS, act)
 
     index_copy.wait()
 
@@ -526,53 +544,87 @@
         slot = pl.ds(s * MOST, MOST)
         return remote(packed.at[block], out.at[0, slot], out_ssem.at[d], out_rsem.at[d], o, a)
 
-    def give(d, _):
-        o = lax.rem(s + d, n_lon)
-        fill(o)
-        to_owner(o, d).start()
+    part_lon = n_lon // 2
+
+    def give(i, _):
+        other = (s // part_lon + 1 + i // part_lon) % 2
+        o = other * part_lon + lax.rem(s + i, part_lon)
+
+        @pl.when(i != part_lon)
+        def _():
+            fill(o)
+            to_owner(o, lax.rem(o + n_lon - s, n_lon)).start()
+
         return 0
 
-    lax.fori_loop(1, OWNERS, give, 0)
+    lax.fori_loop(0, OWNERS, give, 0)
+
+    @pl.when(yields == 1)
+    def _():
+        pl.semaphore_wait(ready_sem, 3)
+        send_south(1)
+
     fill(s)
     own = pltpu.make_async_copy(packed.at[pl.ds(s * MOST, MOST)], out.at[0, pl.ds(s * MOST, MOST)], own_sem)
     own.start()
+    @pl.when(relay_south == 1)
+    def _():
+        pl.semaphore_wait(ready_sem, 1)
+
+        def act(k_size, k):
+            south_copies(k_size, k)[2].wait_recv()
+            relay_copies(k_size, k)[1].start()
+
+        each_row(1, ITERS, act)
+
     to_west.wait_send()
     to_east.wait_send()
-    ends_north.wait_send()
+
+    @pl.when(fold == 0)
+    def _():
+        for j in range(2):
+            ends_copy("north", j).wait_send()
+
+    @pl.when(fold == 1)
+    def _():
+        ends_mirrored.wait_send()
 
     def drain(k_size, k):
         plain, direct, around = north_copies(k_size, k)
-
-        @pl.when(wrap == 0)
+        split = (wrap == 1) & (k <= RELAYED)
+
+        @pl.when(~split)
         def _():
             plain.wait_send()
 
-        @pl.when(wrap == 1)
+        @pl.when(split)
         def _():
             direct.wait_send()
             around.wait_send()
 
-        @pl.when(has_south == 1)
+        @pl.when(near == 1)
         def _():
             south_copies(k_size, k)[0].wait_send()
 
-        @pl.when(relay_north == 1)
+        @pl.when(far == 1)
+        def _():
+            south_copies(k_size, k)[1].wait_send()
+            south_copies(k_size, k)[2].wait_send()
+
+        @pl.when(relay_south == 1)
+        def _():
+            relay_copies(k_size, k)[1].wait_send()
+
+        @pl.when((relay_north == 1) & (k <= RELAYED))
         def _():
             relay_copies(k_size, k)[0].wait_send()
 
-        @pl.when(relay_south == 1)
-        def _():
-            relay_copies(k_size, k)[1].wait_send()
-
     each_row(1, ITERS, drain)
 
     @pl.when(has_south == 1)
     def _():
-        ends_south.wait_send()
-
-    @pl.when(relay_south == 1)
-    def _():
-        ends_forward.wait_send()
+        for j in range(2):
+            ends_copy("south", j).wait_send()
 
     own.wait()
 
@@ -597,17 +649,15 @@
             vmem((2, TOTAL, RING, LEVELS, WIDTH)),
             vmem((ROWS, TILES, LEVELS, WIDTH)),
             vmem((ITERS, 4, TILES, LEVELS, WIDTH)),
-            vmem((2, PIECES, LEVELS, WIDTH)),
             vmem((2, ROWS // GROUP, PIECES, LEVELS, WIDTH)),
             vmem((ROWS // GROUP, 2, PIECES, LEVELS, WIDTH)),
             vmem((2, 2, PIECES, LEVELS, WIDTH)),
             vmem((OWNERS * MOST, LEVELS, WIDTH)),
-            pltpu.SMEM((ROWS, TILES), jnp.int32),
-            pltpu.VMEM((ROWS, TILES), jnp.int32),
+            pltpu.SMEM((TILES, ROWS), jnp.int32),
             pltpu.VMEM((2 * LEVELS, WIDTH), jnp.int32),
             pltpu.SMEM((2 * LEVELS, WIDTH), jnp.int32),
             dma((ROWS // GROUP + 1,)),
-            dma((2,)),
+            dma((1,)),
             pltpu.SemaphoreType.REGULAR,
             dma((2,)),
             dma((2,)),
@@ -615,8 +665,8 @@
             dma((ITERS,)),
             dma((ITERS,)),
             dma((2, 2, ITERS)),
-            dma((3,)),
-            dma((3,)),
+            dma((3, 2)),
+            dma((3, 2)),
             dma((ITERS,)),
             dma((ITERS,)),
             dma((OWNERS,)),
@@ -625,7 +675,7 @@
             dma,
         ],
         compiler_params=pltpu.CompilerParams(collective_id=0, has_side_effects=True),
-    )(forcing, kappa_lon, kappa_lat, shear, amplitude, tile_owner)
+    )(forcing, kappa_lon, kappa_lat, shear, amplitude, tile_owner.T)
 
 
 def solution(mesh):

time: 46.3 us -> 47 us (1.015)
  the two profiles are of different devices: /device:TPU:6 before, /device:TPU:766 now
where the time goes in v3:
time: 47 us; the launch traced here: 46.7 us
  Pallas kernels  44.9 us (96%)
  local copies, waits for them, and re-layouts  1.77 us (4%)
    pallas_call x1, Pallas kernels, per_device(): pl.pallas_call(kernel, out_shape=jax.ShapeDtypeStruct((1, OWNERS * MOST,...  44.9 us
    unnamed x1, local copies, waits for them, and re-layouts  1.77 us

profile of v3, /device:TPU:766, one launch (start us, length us, event | category | flops | bytes accessed | tf_op | source)
XLA Modules:
  0.0 46.7 jit_solution(13953927622920787275)
XLA Ops:
  0.0 44.9 %shard_map.64 = f32[1,96,8,128]{3,2,1,0:T(8,128)} custom-call(f32[8,24,512]{2,1,0:T(8,128)} %forcing.1, f32[8,24,512]{2,1,0:T(8,128)} %kappa_lon.1, f32[8,24,512]{2,1,0:T(8,128)} %kappa_lat.1, f32[8,24,512]{2,1,0:T(8,128)} %shear.1, f32[8,24,512]{2,1,0:T(8,128)} %amplitude.1, s32[4,24]{1,0:T(4,128)} %bitcast.1), custom_call_target="tpu_custom_call" | custom-call | tf_op jit(solution)/shard_map/pallas_call | solution.py:641
  44.9 1.8 %copy.8 = f32[1,96,8,128]{3,2,1,0:T(8,128)} copy(f32[1,96,8,128]{3,2,1,0:T(8,128)} %shard_map.64) | data formatting | bytes 786432
